TPU v7x, 256 devices: a whole 4x4x8 slice. The times are simulated.
256 devices in a mesh: tm: 8 (over z), space: 16 (over y, x_hi, core), net: 2 (over x_lo).
Axes of the slice: x: 4 (x_hi: 2, x_lo: 2; x = x_hi * 2 + x_lo), y: 4, z: 8, core: 2. Of those that a mesh axis runs over, the one named last changes fastest.
Arguments:
- query_rows: bfloat16 [2, 8, 32, 64, 2560], P('net', 'tm', 'space'), may hold values from -140 to 140
- key_rows: bfloat16 [2, 8, 32, 64, 2560], P('net', 'tm', 'space'), may hold values from -8 to 8
- value_rows: bfloat16 [2, 8, 32, 64, 2560], P('net', 'tm', 'space'), may hold values from -6 to 6
- time_proj: bfloat16 [2, 256, 2560], P('net'), may hold values from -0.375 to 0.375
- block_list: int32 [8, 32, 9], P('tm', 'space'), may hold values from 0 to 255, as said below
- block_count: int32 [8, 32], P('tm', 'space'), may hold values from 1 to 9
- timestep: int32 [1], replicated, may hold values from 0 to 999
Outputs:
- latent_grad: bfloat16 [8, 32, 64, 2560], P('tm', 'space', None, 'net')
Inputs may be any that keep to these rules, and one draw needn't show every extreme that they name: `block_list`: entry (f, b, s) names a block f2 * 32 + b2 with f2 within one of f and b2 within one of b, inside the grid; slot 0 is the query's own block; the first block_count[f, b] entries are distinct; the rest repeat the own block.
All inputs are finite; a program needn't handle non-finite values.
Results may differ from a plain program's by a relative error of at most 0.0053.
Values may be sent and summed in bfloat16 or wider, within the bound.
A program may use at most 64 MiB of HBM per device.

v0:
```python
import jax
import jax.numpy as jnp
from jax import lax
from jax.sharding import PartitionSpec as P

HD = 128
FREQ = 256


def with_halo(block, sides, width):
    for axis, dim in sides:
        count = lax.axis_size(axis)
        forward = [(i, i + 1) for i in range(count - 1)]
        backward = [(target, source) for source, target in forward]
        low = lax.ppermute(
            lax.slice_in_dim(block, block.shape[dim] - width, None, axis=dim), axis, forward
        )
        high = lax.ppermute(lax.slice_in_dim(block, 0, width, axis=dim), axis, backward)
        block = jnp.concatenate([low, block, high], axis=dim)
    return block


def gate_vector(timestep, proj):
    half = FREQ // 2
    freqs = jnp.exp(-jnp.log(jnp.float32(10000.0)) * jnp.arange(half, dtype=jnp.float32) / half)
    angle = timestep[0].astype(jnp.float32) * freqs
    feature = jax.nn.silu(jnp.concatenate([jnp.cos(angle), jnp.sin(angle)])).astype(jnp.bfloat16)
    return jnp.dot(feature[None, :], proj, preferred_element_type=jnp.float32)[0]


def shards(query_rows, key_rows, value_rows, time_proj, block_list, block_count, timestep):
    queries = query_rows[0]
    frames_here, blocks_here, block_len, features = queries.shape
    head_count = features // HD
    stacked = jnp.stack([key_rows[0], value_rows[0]])
    padded = with_halo(stacked, (("tm", 1), ("space", 2)), 1)
    row_width = blocks_here + 2
    flat_blocks = padded.reshape(2, (frames_here + 2) * row_width, block_len, features)
    first_frame = lax.axis_index("tm") * frames_here
    first_block = lax.axis_index("space") * blocks_here
    total_blocks = blocks_here * lax.axis_size("space")
    global_frame = block_list // total_blocks
    global_block = block_list % total_blocks
    local_index = (global_frame - first_frame + 1) * row_width + (global_block - first_block + 1)
    slot_count = block_list.shape[-1]
    rows = frames_here * blocks_here
    local_index = local_index.reshape(rows, slot_count)
    gathered_keys = flat_blocks[0][local_index].reshape(
        rows, slot_count * block_len, head_count, HD
    )
    query_heads = queries.reshape(rows, block_len, head_count, HD)
    scores = jnp.einsum(
        "qihd,qjhd->qhij", query_heads, gathered_keys, preferred_element_type=jnp.float32
    )
    scores = scores * HD ** (-0.5)
    slots = jnp.arange(slot_count, dtype=jnp.int32)
    live = jnp.repeat(slots[None, :] < block_count.reshape(rows, 1), block_len, axis=1)
    scores = jnp.where(live[:, None, None, :], scores, jnp.float32(-1e30))
    top = jnp.max(scores, axis=-1, keepdims=True)
    expo = jnp.where(live[:, None, None, :], jnp.exp(scores - top), jnp.float32(0.0))
    total = jnp.sum(expo, axis=-1)
    weights = expo.astype(jnp.bfloat16)
    gathered_values = flat_blocks[1][local_index].reshape(
        rows, slot_count * block_len, head_count, HD
    )
    mixed = jnp.einsum(
        "qhij,qjhd->qihd", weights, gathered_values, preferred_element_type=jnp.float32
    )
    mixed = mixed / jnp.transpose(total, (0, 2, 1))[..., None]
    attended = mixed.reshape(frames_here, blocks_here, block_len, features)
    gate = gate_vector(timestep, time_proj[0])
    polarity = 2.0 * lax.axis_index("net").astype(jnp.float32) - 1.0
    term = polarity * gate * attended
    return lax.psum_scatter(term, "net", scatter_dimension=3, tiled=True).astype(jnp.bfloat16)


def solution(mesh):
    return jax.shard_map(
        shards,
        mesh=mesh,
        in_specs=(
            P("net", "tm", "space", None, None),
            P("net", "tm", "space", None, None),
            P("net", "tm", "space", None, None),
            P("net", None, None),
            P("tm", "space", None),
            P("tm", "space"),
            P(),
        ),
        out_specs=P("tm", "space", None, "net"),
        check_vma=False,
    )
```

profile of v0, /device:TPU:121, one launch (start us, length us, event | category | flops | bytes accessed | tf_op | source)
XLA Modules:
  0.0 192.6 jit_solution(7698557786282790014)
XLA Ops:
  6.5 1.2 constant_dynamic-update-slice_fusion.1
  7.8 1.1 constant_dynamic-update-slice_fusion
  8.9 4.8 %collective-permute-start = (bf16[2,1,2,64,2560]{4,3,2,1,0:T(8,128)(2,1)S(1)}, bf16[2,1,2,64,2560]{4,3,2,1,0:T(8,128)(2,1)S(1)}, u32[]{:S(2)}, u32[]{:S(2)}) collective-permute-start(bf16[2,1,2,64,2560]{4,3,2,1,0:T(8,128)(2,1)S(1)} %constant_dynamic-update-slice_fusion), channel_id=1, source_target_pairs={{0,32},{32,64},{64,96},{96,128},{128,160},{160,192},{192,224},{1,3... | collective-permute-start | bytes 3932168 | tf_op jit(solution)/shard_map/ppermute | solution.py:15
  13.7 1.9 collective-permute-start.1
  15.6 25.5 %collective-permute-done = bf16[2,1,2,64,2560]{4,3,2,1,0:T(8,128)(2,1)S(1)} collective-permute-done((bf16[2,1,2,64,2560]{4,3,2,1,0:T(8,128)(2,1)S(1)}, bf16[2,1,2,64,2560]{4,3,2,1,0:T(8,128)(2,1)S(1)}, u32[]{:S(2)}, u32[]{:S(2)}) %collective-permute-start) | collective-permute-done | bytes 1310752 | tf_op jit(solution)/shard_map/ppermute | solution.py:15
  41.1 5.0 %collective-permute-done.1 = bf16[2,1,2,64,2560]{4,3,2,1,0:T(8,128)(2,1)S(1)} collective-permute-done((bf16[2,1,2,64,2560]{4,3,2,1,0:T(8,128)(2,1)S(1)}, bf16[2,1,2,64,2560]{4,3,2,1,0:T(8,128)(2,1)S(1)}, u32[]{:S(2)}, u32[]{:S(2)}) %collective-permute-start.1) | collective-permute-done | bytes 1310752 | tf_op jit(solution)/shard_map/ppermute | solution.py:18
  47.7 2.2 %fusion.37 = (bf16[2,3,1,64,2560]{4,3,2,1,0:T(8,128)(2,1)}, bf16[2,3,1,64,2560]{4,3,2,1,0:T(8,128)(2,1)}) fusion(bf16[2,3,2,64,2560]{4,3,2,1,0:T(8,128)(2,1)S(1)} %pad_maximum_fusion.1), kind=kLoop, calls=%fused_computation.47 | loop fusion | bytes 7864320 | tf_op jit(solution)/shard_map/slice | solution.py:16
  49.9 6.4 %collective-permute-start.2 = (bf16[2,3,1,64,2560]{4,3,2,1,0:T(8,128)(2,1)}, bf16[2,3,1,64,2560]{4,3,2,1,0:T(8,128)(2,1)}, u32[]{:S(2)}, u32[]{:S(2)}) collective-permute-start(bf16[2,3,1,64,2560]{4,3,2,1,0:T(8,128)(2,1)} %get-tuple-element.7), channel_id=1, source_target_pairs={{0,2},{2,4},{4,6},{6,8},{8,10},{10,12},{12,14},{14,16},{16,18},{18... | collective-permute-start | bytes 5898248 | tf_op jit(solution)/shard_map/ppermute | solution.py:15
  56.3 1.9 collective-permute-start.3
  58.3 1.5 reshape_squeeze.3
  61.2 34.4 %collective-permute-done.2 = bf16[2,3,1,64,2560]{4,3,2,1,0:T(8,128)(2,1)} collective-permute-done((bf16[2,3,1,64,2560]{4,3,2,1,0:T(8,128)(2,1)}, bf16[2,3,1,64,2560]{4,3,2,1,0:T(8,128)(2,1)}, u32[]{:S(2)}, u32[]{:S(2)}) %collective-permute-start.2) | collective-permute-done | bytes 1966112 | tf_op jit(solution)/shard_map/ppermute | solution.py:15
  95.5 3.9 %pad_maximum_fusion = bf16[2,3,4,64,2560]{4,3,2,1,0:T(8,128)(2,1)S(1)} fusion(bf16[2,3,1,64,2560]{4,3,2,1,0:T(8,128)(2,1)} %collective-permute-done.3, bf16[2,1,2,64,2560]{4,3,2,1,0:T(8,128)(2,1)} %copy-done.3, bf16[2,1,2,64,2560]{4,3,2,1,0:T(8,128)(2,1)S(1)} %constant_dynamic-update-slice_fusion, bf16[2,1,2,64,2560]{4,3,2,1,0:T(8,128)(2,1)} %copy-done.2, ...), kind=kLoop, calls=%fused_computation.3 | loop fusion | flops 15728640 | bytes 15728640 | tf_op jit(solution)/shard_map/concatenate | solution.py:19
  99.5 3.4 %fusion.36 = (bf16[1,3,4,64,2560]{4,3,2,1,0:T(8,128)(2,1)}, bf16[1,3,4,64,2560]{4,3,2,1,0:T(8,128)(2,1)}) fusion(bf16[2,3,4,64,2560]{4,3,2,1,0:T(8,128)(2,1)S(1)} %pad_maximum_fusion), kind=kLoop, calls=%fused_computation.46 | loop fusion | bytes 15728640 | tf_op jit(solution)/shard_map/slice | solution.py:48
  102.9 6.6 %gather_fusion.1 = bf16[18,64,2560]{2,1,0:T(8,128)(2,1)} fusion(bf16[12,64,2560]{2,1,0:T(8,128)(2,1)} %bitcast.36, s32[1024]{0:T(1024)S(1)} %pad_clamp_fusion), kind=kCustom, calls=%fused_computation.1 | custom fusion | bytes 11796552 | tf_op jit(solution)/shard_map/gather | solution.py:48
  109.5 10.8 %reshape.79 = bf16[2,576,20,128]{3,2,1,0:T(8,128)(2,1)} reshape(bf16[18,64,2560]{2,1,0:T(8,128)(2,1)} %gather_fusion.1) | data formatting | bytes 11796480 | tf_op jit(solution)/shard_map/reshape | solution.py:48
  120.3 6.6 %gather_fusion = bf16[18,64,2560]{2,1,0:T(8,128)(2,1)} fusion(bf16[12,64,2560]{2,1,0:T(8,128)(2,1)} %bitcast.35, s32[1024]{0:T(1024)S(1)} %pad_clamp_fusion), kind=kCustom, calls=%fused_computation | custom fusion | bytes 11796552 | tf_op jit(solution)/shard_map/gather | solution.py:63
  126.9 10.8 %reshape.78 = bf16[2,576,20,128]{3,2,1,0:T(8,128)(2,1)} reshape(bf16[18,64,2560]{2,1,0:T(8,128)(2,1)} %gather_fusion) | data formatting | bytes 11796480 | tf_op jit(solution)/shard_map/reshape | solution.py:63
  137.7 5.4 %fusion.6 = f32[2,20,576,64]{2,3,1,0:T(8,128)S(1)} fusion(bf16[2,576,20,128]{3,2,1,0:T(8,128)(2,1)} %reshape.79, bf16[2,64,20,128]{3,2,1,0:T(8,128)(2,1)S(1)} %reshape_squeeze.3), kind=kOutput, calls=%fused_computation.12 | convolution fusion | flops 377487360 | bytes 12451840 | tf_op jit(solution)/shard_map/qihd,qjhd->qhij/dot_general | solution.py:52
  143.1 2.7 %fusion.38 = (f32[2,20,64]{2,1,0:T(8,128)S(1)}, bf16[2,20,64,576]{3,2,1,0:T(8,128)(2,1)S(1)}) fusion(f32[2,20,576,64]{2,3,1,0:T(8,128)S(1)} %fusion.6, pred[2,576]{1,0:T(4,128)(4,1)S(1)} %broadcast_in_dim.33), kind=kOutput, calls=%fused_computation.48 | output fusion | flops 11797055 | bytes 8858752 | tf_op jit(solution)/shard_map/sub | solution.py:60
  145.9 1.5 fusion.24
  148.2 1.3 reshape.80
  149.4 2.5 %broadcast_multiply_fusion = f32[1,2,64,2560]{3,2,1,0:T(8,128)} fusion(f32[1,2,64,2560]{3,2,1,0:T(8,128)} %reshape.80, f32[2560]{0:T(1024)S(1)} %broadcast_multiply_fusion.1), kind=kLoop, calls=%fused_computation.25 | loop fusion | flops 327680 | bytes 2631680 | tf_op jit(solution)/shard_map/mul | solution.py:73
  152.0 31.9 %reduce-scatter.2.cloned.1.call-done = f32[1,2,64,1280]{3,2,1,0:T(8,128)} async-done(((f32[1,2,64,2560]{3,2,1,0:T(8,128)}), f32[1,2,64,1280]{3,2,1,0:T(8,128)}) %reduce-scatter.2.cloned.1.call-update) | async-done | bytes 655376 | tf_op jit(solution)/shard_map/reduce_scatter | solution.py:74
  183.9 1.8 convert_element_type.25
  (33 shorter events, 3.1 us)
Async XLA Ops:
  6.5 54.3 %copy-start = (bf16[1,256,2560]{2,1,0:T(8,128)(2,1)S(1)}, bf16[1,256,2560]{2,1,0:T(8,128)(2,1)}, u32[]{:S(2)}) copy-start(bf16[1,256,2560]{2,1,0:T(8,128)(2,1)} %param.10) | copy-start | bytes 3932164
  6.5 177.4 %reduce-scatter.2.cloned.1.call-start = ((), (), s32[]{:S(2)}) async-start(), calls=%async_computation.1 | async-start | bytes 1966080 | tf_op jit(solution)/shard_map/reduce_scatter | solution.py:74
  8.9 32.2 %collective-permute-start = (bf16[2,1,2,64,2560]{4,3,2,1,0:T(8,128)(2,1)S(1)}, bf16[2,1,2,64,2560]{4,3,2,1,0:T(8,128)(2,1)S(1)}, u32[]{:S(2)}, u32[]{:S(2)}) collective-permute-start(bf16[2,1,2,64,2560]{4,3,2,1,0:T(8,128)(2,1)S(1)} %constant_dynamic-update-slice_fusion), channel_id=1, source_target_pairs={{0,32},{32,64},{64,96},{96,128},{128,160},{160,192},{192,224},{1,3... | collective-permute-start | bytes 3932168 | tf_op jit(solution)/shard_map/ppermute | solution.py:15
  13.7 32.4 %collective-permute-start.1 = (bf16[2,1,2,64,2560]{4,3,2,1,0:T(8,128)(2,1)S(1)}, bf16[2,1,2,64,2560]{4,3,2,1,0:T(8,128)(2,1)S(1)}, u32[]{:S(2)}, u32[]{:S(2)}) collective-permute-start(bf16[2,1,2,64,2560]{4,3,2,1,0:T(8,128)(2,1)S(1)} %constant_dynamic-update-slice_fusion), channel_id=1, source_target_pairs={{32,0},{64,32},{96,64},{128,96},{160,128},{192,160},{224,192},{33,... | collective-permute-start | bytes 3932168 | tf_op jit(solution)/shard_map/ppermute | solution.py:18
  41.1 5.0 %copy-start.2 = (bf16[2,1,2,64,2560]{4,3,2,1,0:T(8,128)(2,1)}, bf16[2,1,2,64,2560]{4,3,2,1,0:T(8,128)(2,1)S(1)}, u32[]{:S(2)}) copy-start(bf16[2,1,2,64,2560]{4,3,2,1,0:T(8,128)(2,1)S(1)} %collective-permute-done) | copy-start | bytes 3932164
  46.1 1.1 copy-start.3
  47.7 10.6 %copy-start.4 = (s32[1,2,9]{2,1,0:T(2,128)S(1)}, s32[1,2,9]{2,1,0:T(2,128)}, u32[]{:S(2)}) copy-start(s32[1,2,9]{2,1,0:T(2,128)} %param.11) | copy-start | bytes 220
  47.7 12.2 %copy-start.5 = (s32[1,2]{1,0:T(1,128)S(1)}, s32[1,2]{1,0:T(1,128)}, u32[]{:S(2)}) copy-start(s32[1,2]{1,0:T(1,128)} %param.12) | copy-start | bytes 28
  49.9 45.6 %collective-permute-start.2 = (bf16[2,3,1,64,2560]{4,3,2,1,0:T(8,128)(2,1)}, bf16[2,3,1,64,2560]{4,3,2,1,0:T(8,128)(2,1)}, u32[]{:S(2)}, u32[]{:S(2)}) collective-permute-start(bf16[2,3,1,64,2560]{4,3,2,1,0:T(8,128)(2,1)} %get-tuple-element.7), channel_id=1, source_target_pairs={{0,2},{2,4},{4,6},{6,8},{8,10},{10,12},{12,14},{14,16},{16,18},{18... | collective-permute-start | bytes 5898248 | tf_op jit(solution)/shard_map/ppermute | solution.py:15
  56.3 39.3 %collective-permute-start.3 = (bf16[2,3,1,64,2560]{4,3,2,1,0:T(8,128)(2,1)}, bf16[2,3,1,64,2560]{4,3,2,1,0:T(8,128)(2,1)}, u32[]{:S(2)}, u32[]{:S(2)}) collective-permute-start(bf16[2,3,1,64,2560]{4,3,2,1,0:T(8,128)(2,1)} %get-tuple-element.8), channel_id=1, source_target_pairs={{2,0},{4,2},{6,4},{8,6},{10,8},{12,10},{14,12},{16,14},{18,16},{20... | collective-permute-start | bytes 5898248 | tf_op jit(solution)/shard_map/ppermute | solution.py:18
  137.7 8.1 %slice-start = ((s8[7077888]{0:T(1024)(128)(4,1)}), s8[2883584]{0:T(1024)(128)(4,1)S(1)}, s32[]{:S(2)}) async-start(s8[7077888]{0:T(1024)(128)(4,1)} %bitcast.37), calls=%async_computation.2 | async-start | bytes 5767168
  143.1 2.8 %slice-start.1 = ((s8[7077888]{0:T(1024)(128)(4,1)}), s8[4194304]{0:T(1024)(128)(4,1)S(1)}, s32[]{:S(2)}) async-start(s8[7077888]{0:T(1024)(128)(4,1)} %bitcast.37), calls=%async_computation.3 | async-start | bytes 8388608
  147.4 38.4 %copy-start.1 = (bf16[1,256,2560]{2,1,0:T(8,128)(2,1)S(1)}, bf16[1,256,2560]{2,1,0:T(8,128)(2,1)}, u32[]{:S(2)}) copy-start(bf16[1,256,2560]{2,1,0:T(8,128)(2,1)} %param.10) | copy-start | bytes 3932164
Sparse Core Ops, SparseCore 0:
  152.1 31.7 reduce-scatter.1
where the time goes:
time: 196 us; the launch traced here: 193 us
  waiting for transfers between devices  96.8 us (49%)
  local copies, waits for them, and re-layouts  47.7 us (24%)
  starting transfers between devices  15 us (8%)
  between operations  14.3 us (7%)
  other arithmetic  11.7 us (6%)
  matrix products  7.16 us (4%)
    ppermute x2, waiting for transfers between devices, with_halo(): lax.ppermute(lax.slice_in_dim(block, block.shape[dim] - width, None, axis...  59.9 us
    reduce_scatter x1, waiting for transfers between devices, shards(): lax.psum_scatter(term, 'net', scatter_dimension=3, tiled=True)  31.9 us
    ppermute x2, starting transfers between devices, with_halo(): lax.ppermute(lax.slice_in_dim(block, block.shape[dim] - width, None, axis...  11.1 us
    reshape x1, local copies, waits for them, and re-layouts, shards(): flat_blocks[1][local_index]  10.8 us
    reshape x1, local copies, waits for them, and re-layouts, shards(): flat_blocks[0][local_index]  10.8 us
    gather x1, local copies, waits for them, and re-layouts, shards(): flat_blocks[0][local_index]  6.63 us
    gather x1, local copies, waits for them, and re-layouts, shards(): flat_blocks[1][local_index]  6.6 us
    dot_general x1, matrix products, shards(): jnp.einsum('qihd,qjhd->qhij', query_heads, gathered_keys, preferred_eleme...  5.36 us
  transfers between devices with their start and end apart: 5, of which 4 were waited for; matrix products, arithmetic and copies ran while one was open for 1% of the time, Pallas kernels for 0%

commit v1 on v0

v1 whole, which is shorter than its diff:
```python
import functools
import math

import jax
import jax.numpy as jnp
from jax import lax
from jax.experimental import pallas as pl
from jax.experimental.pallas import tpu as pltpu
from jax.sharding import PartitionSpec as P

HD = 128
FREQ = 256
DEAD = -1e30
RATE = HD**-0.5 * math.log2(math.e)
MESH = pl.DeviceIdType.MESH


def kernel(
    chunk,
    block_list,
    block_count,
    timestep,
    q_in,
    k_in,
    v_in,
    proj_in,
    out,
    queries,
    keys,
    values,
    proj,
    gate,
    bias,
    bias_out,
    own_mix,
    own_top,
    own_sum,
    edge_mix,
    edge_stat,
    back_mix,
    back_stat,
    net_out,
    net_in,
    result,
    local_sem,
    result_sem,
    bias_send,
    bias_recv,
    k_send,
    k_recv,
    v_send,
    v_recv,
    q_send,
    q_recv,
    mix_send,
    mix_recv,
    stat_send,
    stat_recv,
    net_send,
    net_recv,
):
    block_len, features = q_in.shape[-2:]
    heads = features // HD
    steps = heads // chunk
    half = steps // 2
    width = chunk * HD
    frames, spaces = lax.axis_size("tm"), lax.axis_size("space")
    frame, space, net = lax.axis_index("tm"), lax.axis_index("space"), lax.axis_index("net")
    up = {"tm": lax.rem(frame + 1, frames)}
    down = {"tm": lax.rem(frame + frames - 1, frames)}
    right = {"space": lax.rem(space + 1, spaces)}
    left = {"space": lax.rem(space + spaces - 1, spaces)}
    other = {"net": 1 - net}

    own_copies = [
        pltpu.make_async_copy(proj_in.at[0], proj, local_sem.at[0]),
        pltpu.make_async_copy(q_in.at[0, 0], queries.at[pl.ds(1, 2)], local_sem.at[1]),
        pltpu.make_async_copy(k_in.at[0, 0], keys.at[1], local_sem.at[2]),
        pltpu.make_async_copy(v_in.at[0, 0], values.at[1], local_sem.at[3]),
    ]
    for copy in own_copies:
        copy.start()

    barrier = pltpu.get_barrier_semaphore()
    for peer in (up, down, left, right, other):
        pl.semaphore_signal(barrier, inc=1, device_id=peer, device_id_type=MESH)
    pl.semaphore_wait(barrier, 5)

    def send(src, dst, send_sem, recv_sem, peer):
        return pltpu.make_async_remote_copy(
            src_ref=src,
            dst_ref=dst,
            send_sem=send_sem,
            recv_sem=recv_sem,
            device_id=peer,
            device_id_type=MESH,
        )

    def lanes(step):
        first = lax.rem((1 - net) * (heads // 2) + step * chunk, heads)
        return pl.ds(pl.multiple_of(first * HD, HD), width)

    def half_lanes(step):
        return pl.ds(pl.multiple_of(step * width, HD), width)

    def arrivals(step):
        at = lanes(step)
        copies = []
        for way, peer, slot in ((0, up, 0), (1, down, 2)):
            copies.append(
                send(
                    k_in.at[0, 0, :, :, at],
                    keys.at[slot, :, :, at],
                    k_send.at[step, way],
                    k_recv.at[step, way],
                    peer,
                )
            )
            copies.append(
                send(
                    v_in.at[0, 0, :, :, at],
                    values.at[slot, :, :, at],
                    v_send.at[step, way],
                    v_recv.at[step, way],
                    peer,
                )
            )
        for way, peer, slot in ((0, left, 3), (1, right, 0)):
            copies.append(
                send(
                    q_in.at[0, 0, way, :, at],
                    queries.at[slot, :, at],
                    q_send.at[step, way],
                    q_recv.at[step, way],
                    peer,
                )
            )
        return copies

    def returns(step):
        at = lanes(step)
        copies = []
        for edge, peer in ((0, left), (1, right)):
            copies.append(
                send(
                    edge_mix.at[edge, :, at],
                    back_mix.at[1 - edge, :, at],
                    mix_send.at[step, edge],
                    mix_recv.at[step, edge],
                    peer,
                )
            )
            copies.append(
                send(
                    edge_stat.at[step, edge],
                    back_stat.at[step, 1 - edge],
                    stat_send.at[step, edge],
                    stat_recv.at[step, edge],
                    peer,
                )
            )
        return copies

    def crossing(step):
        at = half_lanes(step)
        return send(
            net_out.at[:, at], net_in.at[:, at], net_send.at[step], net_recv.at[step], other
        )

    def leaving(step):
        at = half_lanes(step)
        return pltpu.make_async_copy(
            result.at[:, :, at], out.at[0, :, :, at], result_sem.at[step]
        )

    @pl.loop(0, steps)
    def _(step):
        for copy in arrivals(step):
            copy.start()

    column = lax.broadcasted_iota(jnp.int32, (8, 6 * block_len), 1) // block_len
    slots = block_list.shape[-1]

    def listed(row, frame_step, block_step):
        total = 2 * spaces
        wanted = (frame + frame_step) * total + 2 * space + row + block_step
        found = jnp.int32(0)
        for slot in range(slots):
            hit = (block_list[0, row, slot] == wanted) & (slot < block_count[0, row])
            found = found | hit.astype(jnp.int32)
        return jnp.where(found > 0, jnp.float32(0.0), jnp.float32(DEAD))

    def bias_row(entries):
        row = jnp.full(column.shape, DEAD, jnp.float32)
        for place, entry in entries:
            row = jnp.where(column == place, entry, row)
        return row

    for row in range(2):
        bias[1 + row] = bias_row(
            [
                (2 * f + b, listed(row, f - 1, b - row))
                for f in range(3)
                for b in range(2)
            ]
        )
    bias_out[0] = bias_row([(2 * f + 1, listed(0, f - 1, -1)) for f in range(3)])
    bias_out[1] = bias_row([(2 * f, listed(1, f - 1, 1)) for f in range(3)])
    bias_copies = [
        send(bias_out.at[0], bias.at[3], bias_send.at[0], bias_recv.at[0], left),
        send(bias_out.at[1], bias.at[0], bias_send.at[1], bias_recv.at[1], right),
    ]
    for copy in bias_copies:
        copy.start()

    order = lax.broadcasted_iota(jnp.int32, (8, FREQ // 2), 1).astype(jnp.float32)
    rates = jnp.exp(-jnp.log(jnp.full_like(order, 10000.0)) * order / (FREQ // 2))
    angle = timestep[0].astype(jnp.float32) * rates
    feature = jnp.concatenate([jnp.cos(angle), jnp.sin(angle)], axis=1)
    feature = (feature / (1.0 + jnp.exp(-feature))).astype(jnp.bfloat16)
    polarity = 2.0 * net.astype(jnp.float32) - 1.0
    for copy in own_copies:
        copy.wait()

    @pl.loop(0, heads)
    def _(head):
        at = pl.ds(pl.multiple_of(head * HD, HD), HD)
        gate[:, at] = polarity * jnp.dot(
            feature, proj[:, at], preferred_element_type=jnp.float32
        )

    for copy in bias_copies:
        copy.wait()

    rows = 2 * block_len

    def attend(step):
        for copy in arrivals(step):
            copy.wait_recv()
        start = lanes(step).start
        for j in range(chunk):
            at = pl.ds(pl.multiple_of(start + j * HD, HD), HD)
            q = queries[:, :, at].reshape(4 * block_len, HD)
            k = keys[:, :, :, at].reshape(6 * block_len, HD)
            v = values[:, :, :, at].reshape(6 * block_len, HD)
            scores = lax.dot_general(
                q, k, (((1,), (1,)), ((), ())), preferred_element_type=jnp.float32
            )
            scores = scores.reshape(4, block_len // 8, 8, 6 * block_len) + bias[...][:, None]
            scores = scores.reshape(4 * block_len, 6 * block_len)
            top = jnp.max(scores, axis=-1, keepdims=True)
            expo = jnp.exp2((scores - top) * RATE)
            total = jnp.sum(expo, axis=-1, keepdims=True)
            mix = jnp.dot(expo.astype(jnp.bfloat16), v, preferred_element_type=jnp.float32)
            edge_mix[0, :, at] = mix[:block_len].astype(jnp.bfloat16)
            edge_mix[1, :, at] = mix[3 * block_len :].astype(jnp.bfloat16)
            edge_stat[step, 0, :, j : j + 1] = top[:block_len]
            edge_stat[step, 1, :, j : j + 1] = top[3 * block_len :]
            edge_stat[step, 0, :, 64 + j : 65 + j] = total[:block_len]
            edge_stat[step, 1, :, 64 + j : 65 + j] = total[3 * block_len :]
            own_mix[:, at] = mix[block_len : 3 * block_len]
            own_top[step, j] = top[block_len : 3 * block_len]
            own_sum[step, j] = total[block_len : 3 * block_len]
        for copy in returns(step):
            copy.start()

    def combine(step):
        for copy in returns(step):
            copy.wait_recv()
        start = lanes(step).start

        def term(j):
            at = pl.ds(pl.multiple_of(start + j * HD, HD), HD)
            stat = back_stat[step].reshape(rows, HD)
            top, more_top = own_top[step, j], stat[:, j : j + 1]
            total, more_total = own_sum[step, j], stat[:, 64 + j : 65 + j]
            new_top = jnp.maximum(top, more_top)
            keep = jnp.exp2((top - new_top) * RATE)
            more = jnp.exp2((more_top - new_top) * RATE)
            whole = keep * total + more * more_total
            mixed = own_mix[:, at] * (keep / whole) + back_mix[:, :, at].reshape(
                rows, HD
            ).astype(jnp.float32) * (more / whole)
            gates = gate[:, at]
            return (mixed.reshape(rows // 8, 8, HD) * gates[None]).reshape(rows, HD)

        @pl.when(step < half)
        def _():
            for j in range(chunk):
                at = pl.ds(pl.multiple_of(step * width + j * HD, HD), HD)
                net_out[:, at] = term(j).astype(jnp.bfloat16)
            crossing(step).start()

        @pl.when(step >= half)
        def _():
            crossing(step - half).wait_recv()
            for j in range(chunk):
                at = pl.ds(pl.multiple_of((step - half) * width + j * HD, HD), HD)
                full = term(j) + net_in[:, at].astype(jnp.float32)
                result[:, :, at] = full.astype(jnp.bfloat16).reshape(2, block_len, HD)
            leaving(step - half).start()

    @pl.loop(0, steps)
    def _(step):
        attend(step)

        @pl.when(step > 0)
        def _():
            combine(step - 1)

    combine(steps - 1)

    @pl.loop(0, steps)
    def _(step):
        for copy in arrivals(step):
            copy.wait_send()
        for copy in returns(step):
            copy.wait_send()

    @pl.loop(0, half)
    def _(step):
        crossing(step).wait_send()
        leaving(step).wait()


def shards(query_rows, key_rows, value_rows, time_proj, block_list, block_count, timestep, *, chunk):
    block_len, features = query_rows.shape[-2:]
    heads = features // HD
    steps = heads // chunk
    bf16, f32 = jnp.bfloat16, jnp.float32
    vmem, dma = pltpu.VMEM, pltpu.SemaphoreType.DMA
    smem = pl.BlockSpec(memory_space=pltpu.SMEM)
    hbm = pl.BlockSpec(memory_space=pltpu.HBM)
    return pl.pallas_call(
        functools.partial(kernel, chunk),
        out_shape=jax.ShapeDtypeStruct((1, 2, block_len, features // 2), bf16),
        in_specs=[smem, smem, smem, hbm, hbm, hbm, hbm],
        out_specs=hbm,
        scratch_shapes=[
            vmem((4, block_len, features), bf16),
            vmem((3, 2, block_len, features), bf16),
            vmem((3, 2, block_len, features), bf16),
            vmem((FREQ, features), bf16),
            vmem((8, features), f32),
            vmem((4, 8, 6 * block_len), f32),
            vmem((2, 8, 6 * block_len), f32),
            vmem((2 * block_len, features), f32),
            vmem((steps, chunk, 2 * block_len, 1), f32),
            vmem((steps, chunk, 2 * block_len, 1), f32),
            vmem((2, block_len, features), bf16),
            vmem((steps, 2, block_len, HD), f32),
            vmem((2, block_len, features), bf16),
            vmem((steps, 2, block_len, HD), f32),
            vmem((2 * block_len, features // 2), bf16),
            vmem((2 * block_len, features // 2), bf16),
            vmem((2, block_len, features // 2), bf16),
            dma((4,)),
            dma((steps // 2,)),
            dma((2,)),
            dma((2,)),
            dma((steps, 2)),
            dma((steps, 2)),
            dma((steps, 2)),
            dma((steps, 2)),
            dma((steps, 2)),
            dma((steps, 2)),
            dma((steps, 2)),
            dma((steps, 2)),
            dma((steps, 2)),
            dma((steps, 2)),
            dma((steps // 2,)),
            dma((steps // 2,)),
        ],
        compiler_params=pltpu.CompilerParams(
            collective_id=0, has_side_effects=True, vmem_limit_bytes=60 << 20
        ),
        name="radial_attention",
    )(block_list, block_count, timestep, query_rows, key_rows, value_rows, time_proj)


def solution(mesh, chunk=5):
    return jax.shard_map(
        functools.partial(shards, chunk=chunk),
        mesh=mesh,
        in_specs=(
            P("net", "tm", "space", None, None),
            P("net", "tm", "space", None, None),
            P("net", "tm", "space", None, None),
            P("net", None, None),
            P("tm", "space", None),
            P("tm", "space"),
            P(),
        ),
        out_specs=P("tm", "space", None, "net"),
        check_vma=False,
    )
```

time: 196 us -> 51.7 us (0.26)
  the two profiles are of different devices: /device:TPU:121 before, /device:TPU:1 now
where the time goes in v1:
time: 51.7 us; the launch traced here: 51.5 us
  Pallas kernels  49.1 us (95%)
  local copies, waits for them, and re-layouts  1.72 us (3%)
  between operations  0.66 us (1%)
    pallas_call x1, Pallas kernels, shards(): pl.pallas_call(functools.partial(kernel, chunk), out_shape=jax.ShapeDtype...  49.1 us
    unnamed x1, local copies, waits for them, and re-layouts  1.72 us

profile of v1, /device:TPU:1, one launch (start us, length us, event | category | flops | bytes accessed | tf_op | source)
XLA Modules:
  0.0 51.5 jit_solution(18042650360362251383)
XLA Ops:
  0.7 49.1 %radial_attention.1 = bf16[1,2,64,1280]{3,2,1,0:T(8,128)(2,1)} custom-call(s32[1,2,9]{2,1,0:T(2,128)} %block_list.1, s32[1,2]{1,0:T(1,128)} %block_count.1, s32[1]{0:T(128)S(6)} %copy.9.timestep, bf16[1,1,2,64,2560]{4,3,2,1,0:T(8,128)(2,1)} %q_in.1, bf16[1,1,2,64,2560]{4,3,2,1,0:T(8,128)(2,1)} %k_in.1, bf16[1,1,2,64,2560]{4,3,2,1,0:T(8,128)(2,1)} %v_in.1, ...), custom_call_target="tpu_custom_call" | custom-call | tf_op jit(solution)/shard_map/radial_attention/pallas_call | solution.py:334
  49.8 1.7 %copy.10 = bf16[1,2,64,1280]{3,2,1,0:T(8,128)(2,1)} copy(bf16[1,2,64,1280]{3,2,1,0:T(8,128)(2,1)} %radial_attention.1) | data formatting | bytes 655360

commit v2 on v1

v2 whole, which is shorter than its diff:
```python
import functools
import math

import jax
import jax.numpy as jnp
from jax import lax
from jax.experimental import pallas as pl
from jax.experimental.pallas import tpu as pltpu
from jax.sharding import PartitionSpec as P

HD = 128
FREQ = 256
DEAD = -1e30
RATE = HD**-0.5 * math.log2(math.e)
MESH = pl.DeviceIdType.MESH


def kernel(
    chunk,
    block_list,
    block_count,
    timestep,
    q_in,
    k_in,
    v_in,
    proj_in,
    out,
    queries,
    keys,
    values,
    proj,
    gate,
    bias,
    bias_in,
    bias_out,
    own_mix,
    own_top,
    own_sum,
    columns,
    far_mix,
    far_stat,
    back_mix,
    back_stat,
    net_out,
    net_in,
    result,
    local_sem,
    result_sem,
    bias_send,
    bias_recv,
    q_send,
    q_recv,
    k_send,
    k_recv,
    v_send,
    v_recv,
    mix_send,
    mix_recv,
    stat_send,
    stat_recv,
    net_send,
    net_recv,
):
    block_len, features = q_in.shape[-2:]
    heads = features // HD
    steps = heads // chunk
    half = steps // 2
    width = chunk * HD
    rows = 2 * block_len
    frames, spaces = lax.axis_size("tm"), lax.axis_size("space")
    frame, space, net = lax.axis_index("tm"), lax.axis_index("space"), lax.axis_index("net")
    down, has_down = {"tm": frame - 1}, frame > 0
    up, has_up = {"tm": frame + 1}, frame < frames - 1
    left, has_left = {"space": space - 1}, space > 0
    right, has_right = {"space": space + 1}, space < spaces - 1
    other = {"net": 1 - net}

    barrier = pltpu.get_barrier_semaphore()
    peers = ((down, has_down), (up, has_up), (left, has_left), (right, has_right))
    for peer, there in peers:

        @pl.when(there)
        def _():
            pl.semaphore_signal(barrier, inc=1, device_id=peer, device_id_type=MESH)

    pl.semaphore_signal(barrier, inc=1, device_id=other, device_id_type=MESH)

    own_copies = [
        pltpu.make_async_copy(q_in.at[0, 0], queries.at[pl.ds(2, 2)], local_sem.at[0]),
        pltpu.make_async_copy(k_in.at[0, 0], keys.at[pl.ds(1, 2)], local_sem.at[1]),
        pltpu.make_async_copy(v_in.at[0, 0], values.at[pl.ds(1, 2)], local_sem.at[2]),
        pltpu.make_async_copy(proj_in.at[0], proj, local_sem.at[3]),
    ]
    for copy in own_copies:
        copy.start()

    column = lax.broadcasted_iota(jnp.int32, (8, 4 * block_len), 1) // block_len
    sublane = lax.broadcasted_iota(jnp.int32, (8, 4 * block_len), 0)
    slots = block_list.shape[-1]

    def listed(row, frame_step, block_step):
        wanted = (frame + frame_step) * (2 * spaces) + 2 * space + row + block_step
        found = jnp.int32(0)
        for slot in range(slots):
            hit = (block_list[0, row, slot] == wanted) & (slot < block_count[0, row])
            found = found | hit.astype(jnp.int32)
        return jnp.where(found > 0, jnp.float32(0.0), jnp.float32(DEAD))

    def bias_rows(frame_step):
        both = []
        for row in range(2):
            entries = jnp.full(column.shape, DEAD, jnp.float32)
            for place in range(row, row + 3):
                entry = listed(row, frame_step, place - 1 - row)
                entries = jnp.where(column == place, entry, entries)
            both.append(entries)
        return jnp.where(sublane == 0, both[0], both[1])

    bias_out[0] = bias_rows(-1)
    bias_out[1] = bias_rows(1)
    bias_in[1] = bias_rows(0)

    pl.semaphore_wait(barrier, 1 + sum(there.astype(jnp.int32) for _, there in peers))

    def send(src, dst, send_sem, recv_sem, peer):
        return pltpu.make_async_remote_copy(
            src_ref=src,
            dst_ref=dst,
            send_sem=send_sem,
            recv_sem=recv_sem,
            device_id=peer,
            device_id_type=MESH,
        )

    def lanes(step):
        first = lax.rem((1 - net) * (heads // 2) + step * chunk, heads)
        return pl.ds(pl.multiple_of(first * HD, HD), width)

    def half_lanes(step):
        return pl.ds(pl.multiple_of(step * width, HD), width)

    over_z = ((0, down, 2, has_down, has_up), (1, up, 0, has_up, has_down))
    over_space = ((0, left, 3, has_left, has_right), (1, right, 0, has_right, has_left))

    def bias_copies():
        return [
            (
                send(
                    bias_out.at[way], bias_in.at[group], bias_send.at[way], bias_recv.at[way], peer
                ),
                sends,
                receives,
            )
            for way, peer, group, sends, receives in over_z
        ]

    def streams(step):
        at = lanes(step)
        copies = []
        for way, peer, group, sends, receives in over_z:
            copy = send(
                q_in.at[0, 0, :, :, at],
                queries.at[pl.ds(2 * group, 2), :, at],
                q_send.at[step, way],
                q_recv.at[step, way],
                peer,
            )
            copies.append((copy, sends, receives))
        for source, kept, send_sem, recv_sem in (
            (k_in, keys, k_send, k_recv),
            (v_in, values, v_send, v_recv),
        ):
            for way, peer, place, sends, receives in over_space:
                copy = send(
                    source.at[0, 0, way, :, at],
                    kept.at[place, :, at],
                    send_sem.at[step, way],
                    recv_sem.at[step, way],
                    peer,
                )
                copies.append((copy, sends, receives))
        return copies

    def returns(step):
        at = lanes(step)
        copies = []
        for way, peer, _, sends, receives in over_z:
            stat = send(
                far_stat.at[step, way],
                back_stat.at[step, 1 - way],
                stat_send.at[step, way],
                stat_recv.at[step, way],
                peer,
            )
            mix = send(
                far_mix.at[way, :, at],
                back_mix.at[1 - way, :, at],
                mix_send.at[step, way],
                mix_recv.at[step, way],
                peer,
            )
            copies += [(stat, sends, receives), (mix, sends, receives)]
        return copies

    def crossing(step):
        at = half_lanes(step)
        return send(
            net_out.at[:, at], net_in.at[:, at], net_send.at[step], net_recv.at[step], other
        )

    def leaving(step):
        at = half_lanes(step)
        return pltpu.make_async_copy(
            result.at[:, :, at], out.at[0, :, :, at], result_sem.at[step]
        )

    def start_all(copies):
        for copy, sends, _ in copies:
            pl.when(sends)(copy.start)

    def receive_all(copies):
        for copy, _, receives in copies:
            pl.when(receives)(copy.wait_recv)

    def sent_all(copies):
        for copy, sends, _ in copies:
            pl.when(sends)(copy.wait_send)

    start_all(bias_copies())

    @pl.loop(0, steps)
    def _(step):
        start_all(streams(step))

    def edge_copies(block, place):
        return [
            pltpu.make_async_copy(k_in.at[0, 0, block], keys.at[place], local_sem.at[4 + block]),
            pltpu.make_async_copy(v_in.at[0, 0, block], values.at[place], local_sem.at[6 + block]),
        ]

    edges = ((has_left, 0, 0), (has_right, 1, 3))
    for there, block, place in edges:

        @pl.when(jnp.logical_not(there))
        def _():
            for copy in edge_copies(block, place):
                copy.start()

    for there, way in ((has_down, 0), (has_up, 1)):

        @pl.when(jnp.logical_not(there))
        def _():
            for block in range(2):
                queries[4 * way + block] = jnp.zeros((block_len, features), queries.dtype)
            bias_in[2 * way] = jnp.full(bias_in.shape[1:], DEAD, jnp.float32)
            back_mix[way] = jnp.zeros(back_mix.shape[1:], back_mix.dtype)
            kind = lax.broadcasted_iota(jnp.int32, back_stat.shape[2:], 0)
            for step in range(steps):
                back_stat[step, way] = jnp.where(kind < 8, DEAD, 0.0)

    order = lax.broadcasted_iota(jnp.int32, (8, FREQ // 2), 1).astype(jnp.float32)
    rates = jnp.exp(-jnp.log(jnp.full_like(order, 10000.0)) * order / (FREQ // 2))
    angle = timestep[0].astype(jnp.float32) * rates
    feature = jnp.concatenate([jnp.cos(angle), jnp.sin(angle)], axis=1)
    feature = (feature / (1.0 + jnp.exp(-feature))).astype(jnp.bfloat16)
    polarity = 2.0 * net.astype(jnp.float32) - 1.0
    for copy in own_copies:
        copy.wait()
    for there, block, place in edges:

        @pl.when(jnp.logical_not(there))
        def _():
            for copy in edge_copies(block, place):
                copy.wait()

    @pl.loop(0, heads)
    def _(head):
        at = pl.ds(pl.multiple_of(head * HD, HD), HD)
        gate[:, at] = polarity * jnp.dot(
            feature, proj[:, at], preferred_element_type=jnp.float32
        )

    columns[...] = jnp.zeros_like(columns)
    receive_all(bias_copies())
    for group in range(3):
        for row in range(2):
            bias[2 * group + row] = jnp.broadcast_to(
                bias_in[group, row : row + 1, :], bias.shape[1:]
            )

    @pl.loop(0, steps)
    def _(step):
        receive_all(streams(step))
        start = lanes(step).start
        for j in range(chunk):
            at = pl.ds(pl.multiple_of(start + j * HD, HD), HD)
            q = queries[:, :, at].reshape(6 * block_len, HD)
            k = keys[:, :, at].reshape(4 * block_len, HD)
            v = values[:, :, at].reshape(4 * block_len, HD)
            scores = lax.dot_general(
                q, k, (((1,), (1,)), ((), ())), preferred_element_type=jnp.float32
            )
            scores = scores.reshape(6, block_len // 8, 8, 4 * block_len) + bias[...][:, None]
            scores = scores.reshape(6 * block_len, 4 * block_len)
            top = jnp.max(scores, axis=-1, keepdims=True)
            expo = jnp.exp2((scores - top) * RATE)
            total = jnp.sum(expo, axis=-1, keepdims=True)
            mix = jnp.dot(expo.astype(jnp.bfloat16), v, preferred_element_type=jnp.float32)
            for way in range(2):
                far = slice(2 * way * rows, (2 * way + 1) * rows)
                far_mix[way, :, at] = mix[far].astype(jnp.bfloat16)
                columns[way, :, j : j + 1] = top[far]
                columns[way, :, 8 + j : 9 + j] = total[far]
            own_mix[:, at] = mix[rows : 2 * rows]
            own_top[step, j] = top[rows : 2 * rows]
            own_sum[step, j] = total[rows : 2 * rows]
        for way in range(2):
            far_stat[step, way] = columns[way].T[:16]
        start_all(returns(step))

    def combine(step):
        receive_all(returns(step))
        start = lanes(step).start
        stat = back_stat[step].reshape(32, rows)
        stat = jnp.concatenate([stat, jnp.zeros((HD - 32, rows), jnp.float32)], axis=0).T

        def term(j):
            at = pl.ds(pl.multiple_of(start + j * HD, HD), HD)
            tops = [own_top[step, j], stat[:, j : j + 1], stat[:, 16 + j : 17 + j]]
            sums = [own_sum[step, j], stat[:, 8 + j : 9 + j], stat[:, 24 + j : 25 + j]]
            mixes = [own_mix[:, at]] + [back_mix[way, :, at].astype(jnp.float32) for way in (0, 1)]
            top = jnp.maximum(jnp.maximum(tops[0], tops[1]), tops[2])
            scales = [jnp.exp2((t - top) * RATE) for t in tops]
            whole = 1.0 / sum(a * b for a, b in zip(scales, sums))
            mixed = sum(a * (b * whole) for a, b in zip(mixes, scales))
            return (mixed.reshape(rows // 8, 8, HD) * gate[:, at][None]).reshape(rows, HD)

        @pl.when(step < half)
        def _():
            for j in range(chunk):
                at = pl.ds(pl.multiple_of(step * width + j * HD, HD), HD)
                net_out[:, at] = term(j).astype(jnp.bfloat16)
            crossing(step).start()

        @pl.when(step >= half)
        def _():
            crossing(step - half).wait_recv()
            for j in range(chunk):
                at = pl.ds(pl.multiple_of((step - half) * width + j * HD, HD), HD)
                full = term(j) + net_in[:, at].astype(jnp.float32)
                result[:, :, at] = full.astype(jnp.bfloat16).reshape(2, block_len, HD)
            leaving(step - half).start()

    pl.loop(0, steps)(combine)

    sent_all(bias_copies())

    @pl.loop(0, steps)
    def _(step):
        sent_all(streams(step))
        sent_all(returns(step))

    @pl.loop(0, half)
    def _(step):
        crossing(step).wait_send()
        leaving(step).wait()


def shards(query_rows, key_rows, value_rows, time_proj, block_list, block_count, timestep, *, chunk):
    block_len, features = query_rows.shape[-2:]
    heads = features // HD
    steps = heads // chunk
    rows = 2 * block_len
    bf16, f32 = jnp.bfloat16, jnp.float32
    vmem, dma = pltpu.VMEM, pltpu.SemaphoreType.DMA
    smem = pl.BlockSpec(memory_space=pltpu.SMEM)
    hbm = pl.BlockSpec(memory_space=pltpu.HBM)
    pairs = [dma((steps, 2))] * 2
    return pl.pallas_call(
        functools.partial(kernel, chunk),
        out_shape=jax.ShapeDtypeStruct((1, 2, block_len, features // 2), bf16),
        in_specs=[smem, smem, smem, hbm, hbm, hbm, hbm],
        out_specs=hbm,
        scratch_shapes=[
            vmem((6, block_len, features), bf16),
            vmem((4, block_len, features), bf16),
            vmem((4, block_len, features), bf16),
            vmem((FREQ, features), bf16),
            vmem((8, features), f32),
            vmem((6, 8, 4 * block_len), f32),
            vmem((3, 8, 4 * block_len), f32),
            vmem((2, 8, 4 * block_len), f32),
            vmem((rows, features), f32),
            vmem((steps, chunk, rows, 1), f32),
            vmem((steps, chunk, rows, 1), f32),
            vmem((2, rows, HD), f32),
            vmem((2, rows, features), bf16),
            vmem((steps, 2, 16, rows), f32),
            vmem((2, rows, features), bf16),
            vmem((steps, 2, 16, rows), f32),
            vmem((rows, features // 2), bf16),
            vmem((rows, features // 2), bf16),
            vmem((2, block_len, features // 2), bf16),
            dma((8,)),
            dma((steps // 2,)),
            *([dma((2,))] * 2),
            *pairs,
            *pairs,
            *pairs,
            *pairs,
            *pairs,
            *([dma((steps // 2,))] * 2),
        ],
        compiler_params=pltpu.CompilerParams(
            collective_id=0, has_side_effects=True, vmem_limit_bytes=60 << 20
        ),
        name="radial_attention",
    )(block_list, block_count, timestep, query_rows, key_rows, value_rows, time_proj)


def solution(mesh, chunk=5):
    return jax.shard_map(
        functools.partial(shards, chunk=chunk),
        mesh=mesh,
        in_specs=(
            P("net", "tm", "space", None, None),
            P("net", "tm", "space", None, None),
            P("net", "tm", "space", None, None),
            P("net", None, None),
            P("tm", "space", None),
            P("tm", "space"),
            P(),
        ),
        out_specs=P("tm", "space", None, "net"),
        check_vma=False,
    )
```

time: 51.7 us -> 43.5 us (0.84)
  the two profiles are of different devices: /device:TPU:1 before, /device:TPU:121 now
where the time goes in v2:
time: 43.5 us; the launch traced here: 43.3 us
  Pallas kernels  40.9 us (94%)
  local copies, waits for them, and re-layouts  1.72 us (4%)
  between operations  0.66 us (2%)
    pallas_call x1, Pallas kernels, shards(): pl.pallas_call(functools.partial(kernel, chunk), out_shape=jax.ShapeDtype...  40.9 us
    unnamed x1, local copies, waits for them, and re-layouts  1.72 us

profile of v2, /device:TPU:121, one launch (start us, length us, event | category | flops | bytes accessed | tf_op | source)
XLA Modules:
  0.0 43.3 jit_solution(17896972641641992736)
XLA Ops:
  0.7 40.9 %radial_attention.1 = bf16[1,2,64,1280]{3,2,1,0:T(8,128)(2,1)} custom-call(s32[1,2,9]{2,1,0:T(2,128)} %block_list.1, s32[1,2]{1,0:T(1,128)} %block_count.1, s32[1]{0:T(128)S(6)} %copy.9.timestep, bf16[1,1,2,64,2560]{4,3,2,1,0:T(8,128)(2,1)} %q_in.1, bf16[1,1,2,64,2560]{4,3,2,1,0:T(8,128)(2,1)} %k_in.1, bf16[1,1,2,64,2560]{4,3,2,1,0:T(8,128)(2,1)} %v_in.1, ...), custom_call_target="tpu_custom_call" | custom-call | tf_op jit(solution)/shard_map/radial_attention/pallas_call | solution.py:379
  41.6 1.7 %copy.10 = bf16[1,2,64,1280]{3,2,1,0:T(8,128)(2,1)} copy(bf16[1,2,64,1280]{3,2,1,0:T(8,128)(2,1)} %radial_attention.1) | data formatting | bytes 655360

commit v3 on v2

--- a/solution.py
+++ b/solution.py
@@ -17,14 +17,17 @@
 
 def kernel(
     chunk,
-    block_list,
-    block_count,
-    timestep,
+    list_in,
+    count_in,
+    time_in,
     q_in,
     k_in,
     v_in,
     proj_in,
     out,
+    block_list,
+    block_count,
+    timestep,
     queries,
     keys,
     values,
@@ -43,9 +46,7 @@
     back_stat,
     net_out,
     net_in,
-    result,
     local_sem,
-    result_sem,
     bias_send,
     bias_recv,
     q_send,
@@ -85,6 +86,13 @@
 
     pl.semaphore_signal(barrier, inc=1, device_id=other, device_id_type=MESH)
 
+    tables = [
+        pltpu.make_async_copy(list_in, block_list, local_sem.at[8]),
+        pltpu.make_async_copy(count_in, block_count, local_sem.at[9]),
+        pltpu.make_async_copy(time_in, timestep, local_sem.at[10]),
+    ]
+    for copy in tables:
+        copy.start()
     own_copies = [
         pltpu.make_async_copy(q_in.at[0, 0], queries.at[pl.ds(2, 2)], local_sem.at[0]),
         pltpu.make_async_copy(k_in.at[0, 0], keys.at[pl.ds(1, 2)], local_sem.at[1]),
@@ -93,6 +101,9 @@
     ]
     for copy in own_copies:
         copy.start()
+
+    for copy in tables:
+        copy.wait()
 
     column = lax.broadcasted_iota(jnp.int32, (8, 4 * block_len), 1) // block_len
     sublane = lax.broadcasted_iota(jnp.int32, (8, 4 * block_len), 0)
@@ -206,12 +217,6 @@
         at = half_lanes(step)
         return send(
             net_out.at[:, at], net_in.at[:, at], net_send.at[step], net_recv.at[step], other
-        )
-
-    def leaving(step):
-        at = half_lanes(step)
-        return pltpu.make_async_copy(
-            result.at[:, :, at], out.at[0, :, :, at], result_sem.at[step]
         )
 
     def start_all(copies):
@@ -348,8 +353,7 @@
             for j in range(chunk):
                 at = pl.ds(pl.multiple_of((step - half) * width + j * HD, HD), HD)
                 full = term(j) + net_in[:, at].astype(jnp.float32)
-                result[:, :, at] = full.astype(jnp.bfloat16).reshape(2, block_len, HD)
-            leaving(step - half).start()
+                out[0, :, :, at] = full.astype(jnp.bfloat16).reshape(2, block_len, HD)
 
     pl.loop(0, steps)(combine)
 
@@ -363,7 +367,6 @@
     @pl.loop(0, half)
     def _(step):
         crossing(step).wait_send()
-        leaving(step).wait()
 
 
 def shards(query_rows, key_rows, value_rows, time_proj, block_list, block_count, timestep, *, chunk):
@@ -373,15 +376,22 @@
     rows = 2 * block_len
     bf16, f32 = jnp.bfloat16, jnp.float32
     vmem, dma = pltpu.VMEM, pltpu.SemaphoreType.DMA
-    smem = pl.BlockSpec(memory_space=pltpu.SMEM)
     hbm = pl.BlockSpec(memory_space=pltpu.HBM)
+    arrays = (query_rows, key_rows, value_rows, time_proj)
+
+    def stay(array):
+        return pltpu.with_memory_space_constraint(array, pltpu.HBM)
+
     pairs = [dma((steps, 2))] * 2
     return pl.pallas_call(
         functools.partial(kernel, chunk),
         out_shape=jax.ShapeDtypeStruct((1, 2, block_len, features // 2), bf16),
-        in_specs=[smem, smem, smem, hbm, hbm, hbm, hbm],
-        out_specs=hbm,
+        in_specs=[hbm] * 7,
+        out_specs=pl.BlockSpec(memory_space=pltpu.VMEM),
         scratch_shapes=[
+            pltpu.SMEM(block_list.shape, jnp.int32),
+            pltpu.SMEM(block_count.shape, jnp.int32),
+            pltpu.SMEM(timestep.shape, jnp.int32),
             vmem((6, block_len, features), bf16),
             vmem((4, block_len, features), bf16),
             vmem((4, block_len, features), bf16),
@@ -400,9 +410,7 @@
             vmem((steps, 2, 16, rows), f32),
             vmem((rows, features // 2), bf16),
             vmem((rows, features // 2), bf16),
-            vmem((2, block_len, features // 2), bf16),
-            dma((8,)),
-            dma((steps // 2,)),
+            dma((11,)),
             *([dma((2,))] * 2),
             *pairs,
             *pairs,
@@ -412,10 +420,10 @@
             *([dma((steps // 2,))] * 2),
         ],
         compiler_params=pltpu.CompilerParams(
-            collective_id=0, has_side_effects=True, vmem_limit_bytes=60 << 20
+            collective_id=0, has_side_effects=True, vmem_limit_bytes=32 << 20
         ),
         name="radial_attention",
-    )(block_list, block_count, timestep, query_rows, key_rows, value_rows, time_proj)
+    )(stay(block_list), stay(block_count), timestep, *map(stay, arrays))
 
 
 def solution(mesh, chunk=5):

time: 43.5 us -> 41.2 us (0.947)
  Pallas kernels: 40.9 us -> 39.7 us
  local copies, waits for them, and re-layouts: 1.72 us -> 0.73 us
    pallas_call x1, Pallas kernels: 40.9 us -> 39.7 us  [shards(): pl.pallas_call(functools.partial(kernel, chunk), out_shape=jax.ShapeDtype...]
    unnamed x1, local copies, waits for them, and re-layouts: 1.72 us -> 0.73 us
where the time goes in v3:
time: 41.2 us; the launch traced here: 41.1 us
  Pallas kernels  39.7 us (96%)
  local copies, waits for them, and re-layouts  0.73 us (2%)
  between operations  0.66 us (2%)
    pallas_call x1, Pallas kernels, shards(): pl.pallas_call(functools.partial(kernel, chunk), out_shape=jax.ShapeDtype...  39.7 us

profile of v3, /device:TPU:121, one launch (start us, length us, event | category | flops | bytes accessed | tf_op | source)
XLA Modules:
  0.0 41.1 jit_solution(8114371360967872780)
XLA Ops:
  0.7 39.7 %radial_attention.1 = bf16[1,2,64,1280]{3,2,1,0:T(8,128)(2,1)S(1)} custom-call(s32[1,2,9]{2,1,0:T(2,128)} %list_in.1, s32[1,2]{1,0:T(1,128)} %count_in.1, s32[1]{0:T(128)S(6)} %copy.9.time_in, bf16[1,1,2,64,2560]{4,3,2,1,0:T(8,128)(2,1)} %q_in.1, bf16[1,1,2,64,2560]{4,3,2,1,0:T(8,128)(2,1)} %k_in.1, bf16[1,1,2,64,2560]{4,3,2,1,0:T(8,128)(2,1)} %v_in.1, ...), custom_call_target="tpu_custom_call" | custom-call | tf_op jit(solution)/shard_map/radial_attention/pallas_call | solution.py:386
  40.3 0.7 %copy.10 = bf16[1,2,64,1280]{3,2,1,0:T(8,128)(2,1)} copy(bf16[1,2,64,1280]{3,2,1,0:T(8,128)(2,1)S(1)} %radial_attention.1) | data formatting | bytes 655360

commit v4 on v3

--- a/solution.py
+++ b/solution.py
@@ -37,9 +37,9 @@
     bias_in,
     bias_out,
     own_mix,
-    own_top,
-    own_sum,
+    own_stat,
     columns,
+    scales,
     far_mix,
     far_stat,
     back_mix,
@@ -192,26 +192,38 @@
                 copies.append((copy, sends, receives))
         return copies
 
-    def returns(step):
+    def stat_returns(step):
+        return [
+            (
+                send(
+                    far_stat.at[step, way],
+                    back_stat.at[step, 1 - way],
+                    stat_send.at[step, way],
+                    stat_recv.at[step, way],
+                    peer,
+                ),
+                sends,
+                receives,
+            )
+            for way, peer, _, sends, receives in over_z
+        ]
+
+    def mix_returns(step):
         at = lanes(step)
-        copies = []
-        for way, peer, _, sends, receives in over_z:
-            stat = send(
-                far_stat.at[step, way],
-                back_stat.at[step, 1 - way],
-                stat_send.at[step, way],
-                stat_recv.at[step, way],
-                peer,
-            )
-            mix = send(
-                far_mix.at[way, :, at],
-                back_mix.at[1 - way, :, at],
-                mix_send.at[step, way],
-                mix_recv.at[step, way],
-                peer,
-            )
-            copies += [(stat, sends, receives), (mix, sends, receives)]
-        return copies
+        return [
+            (
+                send(
+                    far_mix.at[way, :, at],
+                    back_mix.at[1 - way, :, at],
+                    mix_send.at[step, way],
+                    mix_recv.at[step, way],
+                    peer,
+                ),
+                sends,
+                receives,
+            )
+            for way, peer, _, sends, receives in over_z
+        ]
 
     def crossing(step):
         at = half_lanes(step)
@@ -311,37 +323,48 @@
             expo = jnp.exp2((scores - top) * RATE)
             total = jnp.sum(expo, axis=-1, keepdims=True)
             mix = jnp.dot(expo.astype(jnp.bfloat16), v, preferred_element_type=jnp.float32)
+            for group in range(3):
+                part = slice(group * rows, (group + 1) * rows)
+                columns[group, :, j : j + 1] = top[part]
+                columns[group, :, 8 + j : 9 + j] = total[part]
+            far_mix[0, :, at] = mix[:rows].astype(jnp.bfloat16)
+            own_mix[:, at] = mix[rows : 2 * rows]
+            far_mix[1, :, at] = mix[2 * rows :].astype(jnp.bfloat16)
+        far_stat[step, 0] = columns[0].T[:16]
+        own_stat[step] = columns[1].T[:16]
+        far_stat[step, 1] = columns[2].T[:16]
+        start_all(stat_returns(step))
+        start_all(mix_returns(step))
+
+    def combine(step):
+        start = lanes(step).start
+        receive_all(stat_returns(step))
+        stats = [own_stat[step], back_stat[step, 0], back_stat[step, 1]]
+        top = functools.reduce(jnp.maximum, [stat[:8] for stat in stats])
+        shares = [jnp.exp2((stat[:8] - top) * RATE) for stat in stats]
+        whole = 1.0 / sum(share * stat[8:] for share, stat in zip(shares, stats))
+        shares = [share * whole for share in shares]
+        shares = jnp.concatenate([*shares, jnp.zeros((HD - 24, rows), jnp.float32)], axis=0).T
+
+        def head_lanes(j):
+            return pl.ds(pl.multiple_of(start + j * HD, HD), HD)
+
+        for j in range(chunk):
+            at = head_lanes(j)
+            gates = jnp.broadcast_to(gate[:1, at], (rows, HD))
+            own_mix[:, at] = own_mix[:, at] * (shares[:, j : j + 1] * gates)
             for way in range(2):
-                far = slice(2 * way * rows, (2 * way + 1) * rows)
-                far_mix[way, :, at] = mix[far].astype(jnp.bfloat16)
-                columns[way, :, j : j + 1] = top[far]
-                columns[way, :, 8 + j : 9 + j] = total[far]
-            own_mix[:, at] = mix[rows : 2 * rows]
-            own_top[step, j] = top[rows : 2 * rows]
-            own_sum[step, j] = total[rows : 2 * rows]
-        for way in range(2):
-            far_stat[step, way] = columns[way].T[:16]
-        start_all(returns(step))
-
-    def combine(step):
-        receive_all(returns(step))
-        start = lanes(step).start
-        stat = back_stat[step].reshape(32, rows)
-        stat = jnp.concatenate([stat, jnp.zeros((HD - 32, rows), jnp.float32)], axis=0).T
+                column = 8 + 8 * way + j
+                scales[way, j] = shares[:, column : column + 1] * gates
 
         def term(j):
-            at = pl.ds(pl.multiple_of(start + j * HD, HD), HD)
-            tops = [own_top[step, j], stat[:, j : j + 1], stat[:, 16 + j : 17 + j]]
-            sums = [own_sum[step, j], stat[:, 8 + j : 9 + j], stat[:, 24 + j : 25 + j]]
-            mixes = [own_mix[:, at]] + [back_mix[way, :, at].astype(jnp.float32) for way in (0, 1)]
-            top = jnp.maximum(jnp.maximum(tops[0], tops[1]), tops[2])
-            scales = [jnp.exp2((t - top) * RATE) for t in tops]
-            whole = 1.0 / sum(a * b for a, b in zip(scales, sums))
-            mixed = sum(a * (b * whole) for a, b in zip(mixes, scales))
-            return (mixed.reshape(rows // 8, 8, HD) * gate[:, at][None]).reshape(rows, HD)
+            at = head_lanes(j)
+            parts = [scales[way, j] * back_mix[way, :, at].astype(jnp.float32) for way in (0, 1)]
+            return own_mix[:, at] + parts[0] + parts[1]
 
         @pl.when(step < half)
         def _():
+            receive_all(mix_returns(step))
             for j in range(chunk):
                 at = pl.ds(pl.multiple_of(step * width + j * HD, HD), HD)
                 net_out[:, at] = term(j).astype(jnp.bfloat16)
@@ -350,6 +373,7 @@
         @pl.when(step >= half)
         def _():
             crossing(step - half).wait_recv()
+            receive_all(mix_returns(step))
             for j in range(chunk):
                 at = pl.ds(pl.multiple_of((step - half) * width + j * HD, HD), HD)
                 full = term(j) + net_in[:, at].astype(jnp.float32)
@@ -362,7 +386,8 @@
     @pl.loop(0, steps)
     def _(step):
         sent_all(streams(step))
-        sent_all(returns(step))
+        sent_all(stat_returns(step))
+        sent_all(mix_returns(step))
 
     @pl.loop(0, half)
     def _(step):
@@ -401,9 +426,9 @@
             vmem((3, 8, 4 * block_len), f32),
             vmem((2, 8, 4 * block_len), f32),
             vmem((rows, features), f32),
-            vmem((steps, chunk, rows, 1), f32),
-            vmem((steps, chunk, rows, 1), f32),
-            vmem((2, rows, HD), f32),
+            vmem((steps, 16, rows), f32),
+            vmem((3, rows, HD), f32),
+            vmem((2, chunk, rows, HD), f32),
             vmem((2, rows, features), bf16),
             vmem((steps, 2, 16, rows), f32),
             vmem((2, rows, features), bf16),

time: 41.2 us -> 39.2 us (0.951)
  Pallas kernels: 39.7 us -> 37.7 us
    pallas_call x1, Pallas kernels: 39.7 us -> 37.7 us  [shards(): pl.pallas_call(functools.partial(kernel, chunk), out_shape=jax.ShapeDtype...]
where the time goes in v4:
time: 39.2 us; the launch traced here: 39.1 us
  Pallas kernels  37.7 us (96%)
  local copies, waits for them, and re-layouts  0.73 us (2%)
  between operations  0.66 us (2%)
    pallas_call x1, Pallas kernels, shards(): pl.pallas_call(functools.partial(kernel, chunk), out_shape=jax.ShapeDtype...  37.7 us

profile of v4, /device:TPU:121, one launch (start us, length us, event | category | flops | bytes accessed | tf_op | source)
XLA Modules:
  0.0 39.1 jit_solution(441227512791216614)
XLA Ops:
  0.7 37.7 %radial_attention.1 = bf16[1,2,64,1280]{3,2,1,0:T(8,128)(2,1)S(1)} custom-call(s32[1,2,9]{2,1,0:T(2,128)} %list_in.1, s32[1,2]{1,0:T(1,128)} %count_in.1, s32[1]{0:T(128)S(6)} %copy.9.time_in, bf16[1,1,2,64,2560]{4,3,2,1,0:T(8,128)(2,1)} %q_in.1, bf16[1,1,2,64,2560]{4,3,2,1,0:T(8,128)(2,1)} %k_in.1, bf16[1,1,2,64,2560]{4,3,2,1,0:T(8,128)(2,1)} %v_in.1, ...), custom_call_target="tpu_custom_call" | custom-call | tf_op jit(solution)/shard_map/radial_attention/pallas_call | solution.py:411
  38.3 0.7 %copy.10 = bf16[1,2,64,1280]{3,2,1,0:T(8,128)(2,1)} copy(bf16[1,2,64,1280]{3,2,1,0:T(8,128)(2,1)S(1)} %radial_attention.1) | data formatting | bytes 655360

commit v5 on v4

--- a/solution.py
+++ b/solution.py
@@ -13,6 +13,7 @@
 DEAD = -1e30
 RATE = HD**-0.5 * math.log2(math.e)
 MESH = pl.DeviceIdType.MESH
+AHEAD = 3
 
 
 def kernel(
@@ -44,6 +45,13 @@
     far_stat,
     back_mix,
     back_stat,
+    few_mix,
+    share_out,
+    share_in,
+    pair_out,
+    pair_in,
+    both_out,
+    both_in,
     net_out,
     net_in,
     local_sem,
@@ -59,13 +67,21 @@
     mix_recv,
     stat_send,
     stat_recv,
+    share_send,
+    share_recv,
+    pair_send,
+    pair_recv,
+    both_send,
+    both_recv,
     net_send,
     net_recv,
 ):
     block_len, features = q_in.shape[-2:]
     heads = features // HD
-    steps = heads // chunk
-    half = steps // 2
+    kept = heads // 2
+    few = chunk // 2
+    half = (kept - few) // chunk
+    steps = 1 + 2 * half
     width = chunk * HD
     rows = 2 * block_len
     frames, spaces = lax.axis_size("tm"), lax.axis_size("space")
@@ -143,12 +159,35 @@
             device_id_type=MESH,
         )
 
-    def lanes(step):
-        first = lax.rem((1 - net) * (heads // 2) + step * chunk, heads)
-        return pl.ds(pl.multiple_of(first * HD, HD), width)
-
-    def half_lanes(step):
-        return pl.ds(pl.multiple_of(step * width, HD), width)
+    theirs, ours = (1 - net) * kept * HD, net * kept * HD
+
+    def offset_of(step):
+        return few * HD + lax.rem(step - 1, half) * width
+
+    def first_lane(step):
+        return jnp.where(step <= half, theirs, ours) + offset_of(step)
+
+    def pieces(step):
+        if isinstance(step, int) and step == 0:
+            return [
+                (number, pl.ds(pl.multiple_of(start, HD), few * HD))
+                for number, start in ((0, theirs), (steps, ours))
+            ]
+        return [(step, pl.ds(pl.multiple_of(first_lane(step), HD), width))]
+
+    def head_lanes(step, j):
+        if isinstance(step, int) and step == 0:
+            start = theirs + j * HD if j < few else ours + (j - few) * HD
+        else:
+            start = first_lane(step) + j * HD
+        return pl.ds(pl.multiple_of(start, HD), HD)
+
+    def half_lanes(step, j=None):
+        if isinstance(step, int) and step == 0:
+            return pl.ds(0, few * HD) if j is None else pl.ds(j * HD, HD)
+        if j is None:
+            return pl.ds(pl.multiple_of(offset_of(step), HD), width)
+        return pl.ds(pl.multiple_of(offset_of(step) + j * HD, HD), HD)
 
     over_z = ((0, down, 2, has_down, has_up), (1, up, 0, has_up, has_down))
     over_space = ((0, left, 3, has_left, has_right), (1, right, 0, has_right, has_left))
@@ -165,32 +204,62 @@
             for way, peer, group, sends, receives in over_z
         ]
 
-    def streams(step):
-        at = lanes(step)
-        copies = []
-        for way, peer, group, sends, receives in over_z:
-            copy = send(
-                q_in.at[0, 0, :, :, at],
-                queries.at[pl.ds(2 * group, 2), :, at],
-                q_send.at[step, way],
-                q_recv.at[step, way],
-                peer,
-            )
-            copies.append((copy, sends, receives))
-        for source, kept, send_sem, recv_sem in (
-            (k_in, keys, k_send, k_recv),
-            (v_in, values, v_send, v_recv),
-        ):
-            for way, peer, place, sends, receives in over_space:
-                copy = send(
+    def query_copies(step):
+        return [
+            (
+                send(
+                    q_in.at[0, 0, :, :, at],
+                    queries.at[pl.ds(2 * group, 2), :, at],
+                    q_send.at[number, way],
+                    q_recv.at[number, way],
+                    peer,
+                ),
+                sends,
+                receives,
+            )
+            for number, at in pieces(step)
+            for way, peer, group, sends, receives in over_z
+        ]
+
+    def key_copies(step):
+        return [
+            (
+                send(
                     source.at[0, 0, way, :, at],
-                    kept.at[place, :, at],
-                    send_sem.at[step, way],
-                    recv_sem.at[step, way],
+                    held.at[slot, :, at],
+                    send_sem.at[number, way],
+                    recv_sem.at[number, way],
                     peer,
-                )
-                copies.append((copy, sends, receives))
-        return copies
+                ),
+                sends,
+                receives,
+            )
+            for number, at in pieces(step)
+            for source, held, send_sem, recv_sem in (
+                (k_in, keys, k_send, k_recv),
+                (v_in, values, v_send, v_recv),
+            )
+            for way, peer, slot, sends, receives in over_space
+        ]
+
+    def returning(far, back, send_sem, recv_sem):
+        return [
+            (
+                send(far.at[way], back.at[1 - way], send_sem.at[way], recv_sem.at[way], peer),
+                sends,
+                receives,
+            )
+            for way, peer, _, sends, receives in over_z
+        ]
+
+    def share_copies():
+        return returning(share_out, share_in, share_send, share_recv)
+
+    def both_copies():
+        return returning(both_out, both_in, both_send, both_recv)
+
+    def pair_copy():
+        return send(pair_out, pair_in, pair_send.at[0], pair_recv.at[0], other)
 
     def stat_returns(step):
         return [
@@ -209,7 +278,7 @@
         ]
 
     def mix_returns(step):
-        at = lanes(step)
+        [(_, at)] = pieces(step)
         return [
             (
                 send(
@@ -245,9 +314,13 @@
 
     start_all(bias_copies())
 
-    @pl.loop(0, steps)
+    start_all(query_copies(0) + key_copies(0))
+    for step in range(1, AHEAD):
+        start_all(query_copies(step))
+
+    @pl.loop(1, steps)
     def _(step):
-        start_all(streams(step))
+        start_all(key_copies(step))
 
     def edge_copies(block, place):
         return [
@@ -273,7 +346,9 @@
             back_mix[way] = jnp.zeros(back_mix.shape[1:], back_mix.dtype)
             kind = lax.broadcasted_iota(jnp.int32, back_stat.shape[2:], 0)
             for step in range(steps):
-                back_stat[step, way] = jnp.where(kind < 8, DEAD, 0.0)
+                back_stat[step, way] = jnp.where(kind < 4, DEAD, 0.0)
+            share_in[way] = jnp.zeros(share_in.shape[1:], jnp.float32)
+            both_in[way] = jnp.zeros(both_in.shape[1:], both_in.dtype)
 
     order = lax.broadcasted_iota(jnp.int32, (8, FREQ // 2), 1).astype(jnp.float32)
     rates = jnp.exp(-jnp.log(jnp.full_like(order, 10000.0)) * order / (FREQ // 2))
@@ -305,12 +380,10 @@
                 bias_in[group, row : row + 1, :], bias.shape[1:]
             )
 
-    @pl.loop(0, steps)
-    def _(step):
-        receive_all(streams(step))
-        start = lanes(step).start
+    def attend(step):
+        receive_all(query_copies(step) + key_copies(step))
         for j in range(chunk):
-            at = pl.ds(pl.multiple_of(start + j * HD, HD), HD)
+            at = head_lanes(step, j)
             q = queries[:, :, at].reshape(6 * block_len, HD)
             k = keys[:, :, at].reshape(4 * block_len, HD)
             v = values[:, :, at].reshape(4 * block_len, HD)
@@ -326,78 +399,153 @@
             for group in range(3):
                 part = slice(group * rows, (group + 1) * rows)
                 columns[group, :, j : j + 1] = top[part]
-                columns[group, :, 8 + j : 9 + j] = total[part]
-            far_mix[0, :, at] = mix[:rows].astype(jnp.bfloat16)
+                columns[group, :, 4 + j : 5 + j] = total[part]
             own_mix[:, at] = mix[rows : 2 * rows]
-            far_mix[1, :, at] = mix[2 * rows :].astype(jnp.bfloat16)
-        far_stat[step, 0] = columns[0].T[:16]
-        own_stat[step] = columns[1].T[:16]
-        far_stat[step, 1] = columns[2].T[:16]
+            for way, part in ((0, mix[:rows]), (1, mix[2 * rows :])):
+                if isinstance(step, int) and step == 0:
+                    few_mix[way, :, j * HD : (j + 1) * HD] = part
+                else:
+                    far_mix[way, :, at] = part.astype(jnp.bfloat16)
+        far_stat[step, 0] = columns[0].T[:8]
+        own_stat[step] = columns[1].T[:8]
+        far_stat[step, 1] = columns[2].T[:8]
         start_all(stat_returns(step))
-        start_all(mix_returns(step))
-
-    def combine(step):
-        start = lanes(step).start
+
+    def shares_of(step):
         receive_all(stat_returns(step))
         stats = [own_stat[step], back_stat[step, 0], back_stat[step, 1]]
-        top = functools.reduce(jnp.maximum, [stat[:8] for stat in stats])
-        shares = [jnp.exp2((stat[:8] - top) * RATE) for stat in stats]
-        whole = 1.0 / sum(share * stat[8:] for share, stat in zip(shares, stats))
-        shares = [share * whole for share in shares]
-        shares = jnp.concatenate([*shares, jnp.zeros((HD - 24, rows), jnp.float32)], axis=0).T
-
-        def head_lanes(j):
-            return pl.ds(pl.multiple_of(start + j * HD, HD), HD)
-
+        top = functools.reduce(jnp.maximum, stats)
+        shares = [jnp.exp2((stat - top) * RATE) for stat in stats]
+        sums = [pltpu.roll(stat, 4, 0) for stat in stats]
+        whole = 1.0 / sum(share * total for share, total in zip(shares, sums))
+        return [share * whole for share in shares]
+
+    def upright(tiles):
+        filler = jnp.zeros((HD - 8 * len(tiles), rows), jnp.float32)
+        return jnp.concatenate([*tiles, filler], axis=0).T
+
+    def gates_of(at):
+        return jnp.broadcast_to(gate[:1, at], (rows, HD))
+
+    def tell_shares():
+        shares = shares_of(0)
+        share_out[0] = shares[1]
+        share_out[1] = shares[2]
+        start_all(share_copies())
+        share = upright(shares[:1])
         for j in range(chunk):
-            at = head_lanes(j)
-            gates = jnp.broadcast_to(gate[:1, at], (rows, HD))
+            at = head_lanes(0, j)
+            own = own_mix[:, at] * (share[:, j : j + 1] * gates_of(at))
+            if j < few:
+                net_out[:, half_lanes(0, j)] = own.astype(jnp.bfloat16)
+            else:
+                own_mix[:, at] = own
+        crossing(0).start()
+
+    def exchange_halves():
+        receive_all(share_copies())
+        share = upright([share_in[0], share_in[1]])
+        for way in range(2):
+            for j in range(chunk):
+                column = 8 * way + j
+                here = pl.ds(j * HD, HD)
+                part = few_mix[way, :, here] * (
+                    share[:, column : column + 1] * gates_of(head_lanes(0, j))
+                )
+                if j < few:
+                    pair_out[way, :, here] = part.astype(jnp.bfloat16)
+                else:
+                    few_mix[way, :, here] = part
+        pair_copy().start()
+
+    def return_sums():
+        pair_copy().wait_recv()
+        for way in range(2):
+            both_out[way] = (
+                few_mix[way, :, few * HD :] + pair_in[way].astype(jnp.float32)
+            ).astype(jnp.bfloat16)
+        start_all(both_copies())
+
+    attend(0)
+
+    @pl.loop(1, steps)
+    def _(step):
+        @pl.when(step + AHEAD - 1 < steps)
+        def _():
+            start_all(query_copies(step + AHEAD - 1))
+
+        attend(step)
+        pl.when(step == 1)(tell_shares)
+        start_all(mix_returns(step))
+        pl.when(step == 2)(exchange_halves)
+        pl.when(step == min(3, steps - 1))(return_sums)
+
+    def combine(step):
+        shares = upright(shares_of(step))
+        for j in range(chunk):
+            at = head_lanes(step, j)
+            gates = gates_of(at)
             own_mix[:, at] = own_mix[:, at] * (shares[:, j : j + 1] * gates)
             for way in range(2):
                 column = 8 + 8 * way + j
                 scales[way, j] = shares[:, column : column + 1] * gates
 
         def term(j):
-            at = head_lanes(j)
+            at = head_lanes(step, j)
             parts = [scales[way, j] * back_mix[way, :, at].astype(jnp.float32) for way in (0, 1)]
             return own_mix[:, at] + parts[0] + parts[1]
 
-        @pl.when(step < half)
+        @pl.when(step <= half)
         def _():
             receive_all(mix_returns(step))
             for j in range(chunk):
-                at = pl.ds(pl.multiple_of(step * width + j * HD, HD), HD)
-                net_out[:, at] = term(j).astype(jnp.bfloat16)
+                net_out[:, half_lanes(step, j)] = term(j).astype(jnp.bfloat16)
             crossing(step).start()
 
-        @pl.when(step >= half)
+        @pl.when(step > half)
         def _():
             crossing(step - half).wait_recv()
             receive_all(mix_returns(step))
             for j in range(chunk):
-                at = pl.ds(pl.multiple_of((step - half) * width + j * HD, HD), HD)
+                at = half_lanes(step, j)
                 full = term(j) + net_in[:, at].astype(jnp.float32)
                 out[0, :, :, at] = full.astype(jnp.bfloat16).reshape(2, block_len, HD)
 
-    pl.loop(0, steps)(combine)
+    def combine_few():
+        crossing(0).wait_recv()
+        receive_all(both_copies())
+        for j in range(few):
+            at = half_lanes(0, j)
+            full = own_mix[:, head_lanes(0, few + j)] + net_in[:, at].astype(jnp.float32)
+            for way in range(2):
+                full = full + both_in[way, :, at].astype(jnp.float32)
+            out[0, :, :, at] = full.astype(jnp.bfloat16).reshape(2, block_len, HD)
+
+    pl.loop(1, steps - 1)(combine)
+    combine_few()
+    combine(steps - 1)
 
     sent_all(bias_copies())
 
-    @pl.loop(0, steps)
+    sent_all(query_copies(0) + key_copies(0) + stat_returns(0))
+
+    @pl.loop(1, steps)
     def _(step):
-        sent_all(streams(step))
-        sent_all(stat_returns(step))
-        sent_all(mix_returns(step))
-
-    @pl.loop(0, half)
-    def _(step):
+        sent_all(query_copies(step) + key_copies(step))
+        sent_all(stat_returns(step) + mix_returns(step))
+
+    sent_all(share_copies() + both_copies())
+    pair_copy().wait_send()
+    for step in range(half + 1):
         crossing(step).wait_send()
 
 
 def shards(query_rows, key_rows, value_rows, time_proj, block_list, block_count, timestep, *, chunk):
     block_len, features = query_rows.shape[-2:]
     heads = features // HD
-    steps = heads // chunk
+    few = chunk // 2
+    half = (heads // 2 - few) // chunk
+    steps = 1 + 2 * half
     rows = 2 * block_len
     bf16, f32 = jnp.bfloat16, jnp.float32
     vmem, dma = pltpu.VMEM, pltpu.SemaphoreType.DMA
@@ -408,6 +556,7 @@
         return pltpu.with_memory_space_constraint(array, pltpu.HBM)
 
     pairs = [dma((steps, 2))] * 2
+    pieces = [dma((steps + 1, 2))] * 2
     return pl.pallas_call(
         functools.partial(kernel, chunk),
         out_shape=jax.ShapeDtypeStruct((1, 2, block_len, features // 2), bf16),
@@ -426,23 +575,30 @@
             vmem((3, 8, 4 * block_len), f32),
             vmem((2, 8, 4 * block_len), f32),
             vmem((rows, features), f32),
-            vmem((steps, 16, rows), f32),
+            vmem((steps, 8, rows), f32),
             vmem((3, rows, HD), f32),
             vmem((2, chunk, rows, HD), f32),
             vmem((2, rows, features), bf16),
-            vmem((steps, 2, 16, rows), f32),
+            vmem((steps, 2, 8, rows), f32),
             vmem((2, rows, features), bf16),
-            vmem((steps, 2, 16, rows), f32),
+            vmem((steps, 2, 8, rows), f32),
+            vmem((2, rows, chunk * HD), f32),
+            *([vmem((2, 8, rows), f32)] * 2),
+            *([vmem((2, rows, few * HD), bf16)] * 2),
+            *([vmem((2, rows, few * HD), bf16)] * 2),
             vmem((rows, features // 2), bf16),
             vmem((rows, features // 2), bf16),
             dma((11,)),
             *([dma((2,))] * 2),
+            *pieces,
+            *pieces,
+            *pieces,
             *pairs,
             *pairs,
-            *pairs,
-            *pairs,
-            *pairs,
-            *([dma((steps // 2,))] * 2),
+            *([dma((2,))] * 2),
+            *([dma((1,))] * 2),
+            *([dma((2,))] * 2),
+            *([dma((half + 1,))] * 2),
         ],
         compiler_params=pltpu.CompilerParams(
             collective_id=0, has_side_effects=True, vmem_limit_bytes=32 << 20
@@ -451,7 +607,7 @@
     )(stay(block_list), stay(block_count), timestep, *map(stay, arrays))
 
 
-def solution(mesh, chunk=5):
+def solution(mesh, chunk=4):
     return jax.shard_map(
         functools.partial(shards, chunk=chunk),
         mesh=mesh,

time: 39.2 us -> 38 us (0.969)
  Pallas kernels: 37.7 us -> 36.5 us
    pallas_call x1, Pallas kernels: 37.7 us -> 36.5 us  [shards(): pl.pallas_call(functools.partial(kernel, chunk), out_shape=jax.ShapeDtype...]
where the time goes in v5:
time: 38 us; the launch traced here: 37.9 us
  Pallas kernels  36.5 us (96%)
  local copies, waits for them, and re-layouts  0.73 us (2%)
  between operations  0.66 us (2%)
    pallas_call x1, Pallas kernels, shards(): pl.pallas_call(functools.partial(kernel, chunk), out_shape=jax.ShapeDtype...  36.5 us

profile of v5, /device:TPU:121, one launch (start us, length us, event | category | flops | bytes accessed | tf_op | source)
XLA Modules:
  0.0 37.9 jit_solution(6244467097847752823)
XLA Ops:
  0.7 36.5 %radial_attention.1 = bf16[1,2,64,1280]{3,2,1,0:T(8,128)(2,1)S(1)} custom-call(s32[1,2,9]{2,1,0:T(2,128)} %list_in.1, s32[1,2]{1,0:T(1,128)} %count_in.1, s32[1]{0:T(128)S(6)} %copy.9.time_in, bf16[1,1,2,64,2560]{4,3,2,1,0:T(8,128)(2,1)} %q_in.1, bf16[1,1,2,64,2560]{4,3,2,1,0:T(8,128)(2,1)} %k_in.1, bf16[1,1,2,64,2560]{4,3,2,1,0:T(8,128)(2,1)} %v_in.1, ...), custom_call_target="tpu_custom_call" | custom-call | tf_op jit(solution)/shard_map/radial_attention/pallas_call | solution.py:560
  37.1 0.7 %copy.10 = bf16[1,2,64,1280]{3,2,1,0:T(8,128)(2,1)} copy(bf16[1,2,64,1280]{3,2,1,0:T(8,128)(2,1)S(1)} %radial_attention.1) | data formatting | bytes 655360

commit v6 on v5

--- a/solution.py
+++ b/solution.py
@@ -13,6 +13,7 @@
 DEAD = -1e30
 RATE = HD**-0.5 * math.log2(math.e)
 MESH = pl.DeviceIdType.MESH
+LINES = 4
 AHEAD = 3
 
 
@@ -121,8 +122,8 @@
     for copy in tables:
         copy.wait()
 
-    column = lax.broadcasted_iota(jnp.int32, (8, 4 * block_len), 1) // block_len
-    sublane = lax.broadcasted_iota(jnp.int32, (8, 4 * block_len), 0)
+    column = lax.broadcasted_iota(jnp.int32, (2, 4 * block_len), 1) // block_len
+    sublane = lax.broadcasted_iota(jnp.int32, (2, 4 * block_len), 0)
     slots = block_list.shape[-1]
 
     def listed(row, frame_step, block_step):
@@ -344,9 +345,8 @@
                 queries[4 * way + block] = jnp.zeros((block_len, features), queries.dtype)
             bias_in[2 * way] = jnp.full(bias_in.shape[1:], DEAD, jnp.float32)
             back_mix[way] = jnp.zeros(back_mix.shape[1:], back_mix.dtype)
-            kind = lax.broadcasted_iota(jnp.int32, back_stat.shape[2:], 0)
             for step in range(steps):
-                back_stat[step, way] = jnp.where(kind < 4, DEAD, 0.0)
+                back_stat[step, way] = jnp.full(back_stat.shape[2:], DEAD, jnp.float32)
             share_in[way] = jnp.zeros(share_in.shape[1:], jnp.float32)
             both_in[way] = jnp.zeros(both_in.shape[1:], both_in.dtype)
 
@@ -395,33 +395,35 @@
             top = jnp.max(scores, axis=-1, keepdims=True)
             expo = jnp.exp2((scores - top) * RATE)
             total = jnp.sum(expo, axis=-1, keepdims=True)
+            weight = top * RATE + jnp.log2(total)
             mix = jnp.dot(expo.astype(jnp.bfloat16), v, preferred_element_type=jnp.float32)
+            mix = mix * (1.0 / total)
             for group in range(3):
                 part = slice(group * rows, (group + 1) * rows)
-                columns[group, :, j : j + 1] = top[part]
-                columns[group, :, 4 + j : 5 + j] = total[part]
+                columns[group, :, j : j + 1] = weight[part]
             own_mix[:, at] = mix[rows : 2 * rows]
             for way, part in ((0, mix[:rows]), (1, mix[2 * rows :])):
                 if isinstance(step, int) and step == 0:
                     few_mix[way, :, j * HD : (j + 1) * HD] = part
                 else:
                     far_mix[way, :, at] = part.astype(jnp.bfloat16)
-        far_stat[step, 0] = columns[0].T[:8]
-        own_stat[step] = columns[1].T[:8]
-        far_stat[step, 1] = columns[2].T[:8]
+        far_stat[step, 0] = columns[0].T[:LINES]
+        own_stat[step] = columns[1].T[:LINES]
+        far_stat[step, 1] = columns[2].T[:LINES]
         start_all(stat_returns(step))
 
     def shares_of(step):
         receive_all(stat_returns(step))
-        stats = [own_stat[step], back_stat[step, 0], back_stat[step, 1]]
-        top = functools.reduce(jnp.maximum, stats)
-        shares = [jnp.exp2((stat - top) * RATE) for stat in stats]
-        sums = [pltpu.roll(stat, 4, 0) for stat in stats]
-        whole = 1.0 / sum(share * total for share, total in zip(shares, sums))
+        weights = [own_stat[step], back_stat[step, 0], back_stat[step, 1]]
+        top = functools.reduce(jnp.maximum, weights)
+        shares = [jnp.exp2(weight - top) for weight in weights]
+        whole = 1.0 / sum(shares)
         return [share * whole for share in shares]
 
     def upright(tiles):
-        filler = jnp.zeros((HD - 8 * len(tiles), rows), jnp.float32)
+        filler = jnp.zeros((8 - LINES, rows), jnp.float32)
+        tiles = [piece for tile in tiles for piece in (tile, filler)]
+        filler = jnp.zeros((HD - 4 * len(tiles), rows), jnp.float32)
         return jnp.concatenate([*tiles, filler], axis=0).T
 
     def gates_of(at):
@@ -523,21 +525,24 @@
 
     pl.loop(1, steps - 1)(combine)
     combine_few()
-    combine(steps - 1)
-
-    sent_all(bias_copies())
-
-    sent_all(query_copies(0) + key_copies(0) + stat_returns(0))
+
+    sent_all(bias_copies() + query_copies(0) + key_copies(0) + stat_returns(0))
 
     @pl.loop(1, steps)
     def _(step):
-        sent_all(query_copies(step) + key_copies(step))
-        sent_all(stat_returns(step) + mix_returns(step))
+        sent_all(query_copies(step) + key_copies(step) + stat_returns(step))
 
     sent_all(share_copies() + both_copies())
     pair_copy().wait_send()
     for step in range(half + 1):
         crossing(step).wait_send()
+
+    @pl.loop(1, steps - 1)
+    def _(step):
+        sent_all(mix_returns(step))
+
+    combine(steps - 1)
+    sent_all(mix_returns(steps - 1))
 
 
 def shards(query_rows, key_rows, value_rows, time_proj, block_list, block_count, timestep, *, chunk):
@@ -572,18 +577,18 @@
             vmem((FREQ, features), bf16),
             vmem((8, features), f32),
             vmem((6, 8, 4 * block_len), f32),
-            vmem((3, 8, 4 * block_len), f32),
-            vmem((2, 8, 4 * block_len), f32),
+            vmem((3, 2, 4 * block_len), f32),
+            vmem((2, 2, 4 * block_len), f32),
             vmem((rows, features), f32),
-            vmem((steps, 8, rows), f32),
+            vmem((steps, LINES, rows), f32),
             vmem((3, rows, HD), f32),
             vmem((2, chunk, rows, HD), f32),
             vmem((2, rows, features), bf16),
-            vmem((steps, 2, 8, rows), f32),
+            vmem((steps, 2, LINES, rows), f32),
             vmem((2, rows, features), bf16),
-            vmem((steps, 2, 8, rows), f32),
+            vmem((steps, 2, LINES, rows), f32),
             vmem((2, rows, chunk * HD), f32),
-            *([vmem((2, 8, rows), f32)] * 2),
+            *([vmem((2, LINES, rows), f32)] * 2),
             *([vmem((2, rows, few * HD), bf16)] * 2),
             *([vmem((2, rows, few * HD), bf16)] * 2),
             vmem((rows, features // 2), bf16),

time: 38 us -> 37.6 us (0.989)
  Pallas kernels: 36.5 us -> 36 us
    pallas_call x1, Pallas kernels: 36.5 us -> 36 us  [shards(): pl.pallas_call(functools.partial(kernel, chunk), out_shape=jax.ShapeDtype...]
where the time goes in v6:
time: 37.6 us; the launch traced here: 37.3 us
  Pallas kernels  36 us (96%)
  local copies, waits for them, and re-layouts  0.73 us (2%)
  between operations  0.66 us (2%)
    pallas_call x1, Pallas kernels, shards(): pl.pallas_call(functools.partial(kernel, chunk), out_shape=jax.ShapeDtype...  36 us

profile of v6, /device:TPU:121, one launch (start us, length us, event | category | flops | bytes accessed | tf_op | source)
XLA Modules:
  0.0 37.3 jit_solution(1213344660715415702)
XLA Ops:
  0.7 36.0 %radial_attention.1 = bf16[1,2,64,1280]{3,2,1,0:T(8,128)(2,1)S(1)} custom-call(s32[1,2,9]{2,1,0:T(2,128)} %list_in.1, s32[1,2]{1,0:T(1,128)} %count_in.1, s32[1]{0:T(128)S(6)} %copy.9.time_in, bf16[1,1,2,64,2560]{4,3,2,1,0:T(8,128)(2,1)} %q_in.1, bf16[1,1,2,64,2560]{4,3,2,1,0:T(8,128)(2,1)} %k_in.1, bf16[1,1,2,64,2560]{4,3,2,1,0:T(8,128)(2,1)} %v_in.1, ...), custom_call_target="tpu_custom_call" | custom-call | tf_op jit(solution)/shard_map/radial_attention/pallas_call | solution.py:565
  36.6 0.7 %copy.10 = bf16[1,2,64,1280]{3,2,1,0:T(8,128)(2,1)} copy(bf16[1,2,64,1280]{3,2,1,0:T(8,128)(2,1)S(1)} %radial_attention.1) | data formatting | bytes 655360

commit v7 on v6

--- a/solution.py
+++ b/solution.py
@@ -278,15 +278,18 @@
             for way, peer, _, sends, receives in over_z
         ]
 
-    def mix_returns(step):
-        [(_, at)] = pieces(step)
+    def mix_returns(step, part=None):
+        [(number, at)] = pieces(step)
+        if part is not None:
+            number = (steps - 1, steps)[part]
+            at = pl.ds(pl.multiple_of(first_lane(step) + part * few * HD, HD), few * HD)
         return [
             (
                 send(
                     far_mix.at[way, :, at],
                     back_mix.at[1 - way, :, at],
-                    mix_send.at[step, way],
-                    mix_recv.at[step, way],
+                    mix_send.at[number, way],
+                    mix_recv.at[number, way],
                     peer,
                 ),
                 sends,
@@ -478,7 +481,15 @@
 
         attend(step)
         pl.when(step == 1)(tell_shares)
-        start_all(mix_returns(step))
+
+        @pl.when(step < steps - 1)
+        def _():
+            start_all(mix_returns(step))
+
+        @pl.when(step == steps - 1)
+        def _():
+            start_all(mix_returns(steps - 1, 0) + mix_returns(steps - 1, 1))
+
         pl.when(step == 2)(exchange_halves)
         pl.when(step == min(3, steps - 1))(return_sums)
 
@@ -507,8 +518,12 @@
         @pl.when(step > half)
         def _():
             crossing(step - half).wait_recv()
-            receive_all(mix_returns(step))
+            last = isinstance(step, int) and step == steps - 1
+            if not last:
+                receive_all(mix_returns(step))
             for j in range(chunk):
+                if last and j % few == 0:
+                    receive_all(mix_returns(step, j // few))
                 at = half_lanes(step, j)
                 full = term(j) + net_in[:, at].astype(jnp.float32)
                 out[0, :, :, at] = full.astype(jnp.bfloat16).reshape(2, block_len, HD)
@@ -542,7 +557,7 @@
         sent_all(mix_returns(step))
 
     combine(steps - 1)
-    sent_all(mix_returns(steps - 1))
+    sent_all(mix_returns(steps - 1, 0) + mix_returns(steps - 1, 1))
 
 
 def shards(query_rows, key_rows, value_rows, time_proj, block_list, block_count, timestep, *, chunk):
@@ -598,7 +613,7 @@
             *pieces,
             *pieces,
             *pieces,
-            *pairs,
+            *pieces,
             *pairs,
             *([dma((2,))] * 2),
             *([dma((1,))] * 2),

time: 37.6 us -> 37.6 us (level)
  no operation moved by 1% of the time
where the time goes in v7:
time: 37.6 us; the launch traced here: 37.3 us
  Pallas kernels  35.9 us (95%)
  local copies, waits for them, and re-layouts  0.73 us (2%)
  between operations  0.66 us (2%)
    pallas_call x1, Pallas kernels, shards(): pl.pallas_call(functools.partial(kernel, chunk), out_shape=jax.ShapeDtype...  35.9 us

profile of v7, /device:TPU:121, one launch (start us, length us, event | category | flops | bytes accessed | tf_op | source)
XLA Modules:
  0.0 37.3 jit_solution(13607259630589565586)
XLA Ops:
  0.7 35.9 %radial_attention.1 = bf16[1,2,64,1280]{3,2,1,0:T(8,128)(2,1)S(1)} custom-call(s32[1,2,9]{2,1,0:T(2,128)} %list_in.1, s32[1,2]{1,0:T(1,128)} %count_in.1, s32[1]{0:T(128)S(6)} %copy.9.time_in, bf16[1,1,2,64,2560]{4,3,2,1,0:T(8,128)(2,1)} %q_in.1, bf16[1,1,2,64,2560]{4,3,2,1,0:T(8,128)(2,1)} %k_in.1, bf16[1,1,2,64,2560]{4,3,2,1,0:T(8,128)(2,1)} %v_in.1, ...), custom_call_target="tpu_custom_call" | custom-call | tf_op jit(solution)/shard_map/radial_attention/pallas_call | solution.py:580
  36.6 0.7 %copy.10 = bf16[1,2,64,1280]{3,2,1,0:T(8,128)(2,1)} copy(bf16[1,2,64,1280]{3,2,1,0:T(8,128)(2,1)S(1)} %radial_attention.1) | data formatting | bytes 655360

commit v8 on v7

--- a/solution.py
+++ b/solution.py
@@ -368,13 +368,6 @@
             for copy in edge_copies(block, place):
                 copy.wait()
 
-    @pl.loop(0, heads)
-    def _(head):
-        at = pl.ds(pl.multiple_of(head * HD, HD), HD)
-        gate[:, at] = polarity * jnp.dot(
-            feature, proj[:, at], preferred_element_type=jnp.float32
-        )
-
     columns[...] = jnp.zeros_like(columns)
     receive_all(bias_copies())
     for group in range(3):
@@ -472,6 +465,13 @@
         start_all(both_copies())
 
     attend(0)
+
+    @pl.loop(0, heads)
+    def _(head):
+        at = pl.ds(pl.multiple_of(head * HD, HD), HD)
+        gate[:, at] = polarity * jnp.dot(
+            feature, proj[:, at], preferred_element_type=jnp.float32
+        )
 
     @pl.loop(1, steps)
     def _(step):

time: 37.6 us -> 38.8 us (1.032)
  the two profiles are of different devices: /device:TPU:121 before, /device:TPU:81 now
where the time goes in v8:
time: 38.8 us; the launch traced here: 38.7 us
  Pallas kernels  37.3 us (96%)
  local copies, waits for them, and re-layouts  0.73 us (2%)
  between operations  0.66 us (2%)
    pallas_call x1, Pallas kernels, shards(): pl.pallas_call(functools.partial(kernel, chunk), out_shape=jax.ShapeDtype...  37.3 us

profile of v8, /device:TPU:81, one launch (start us, length us, event | category | flops | bytes accessed | tf_op | source)
XLA Modules:
  0.0 38.7 jit_solution(12037586437168448312)
XLA Ops:
  0.7 37.3 %radial_attention.1 = bf16[1,2,64,1280]{3,2,1,0:T(8,128)(2,1)S(1)} custom-call(s32[1,2,9]{2,1,0:T(2,128)} %list_in.1, s32[1,2]{1,0:T(1,128)} %count_in.1, s32[1]{0:T(128)S(6)} %copy.9.time_in, bf16[1,1,2,64,2560]{4,3,2,1,0:T(8,128)(2,1)} %q_in.1, bf16[1,1,2,64,2560]{4,3,2,1,0:T(8,128)(2,1)} %k_in.1, bf16[1,1,2,64,2560]{4,3,2,1,0:T(8,128)(2,1)} %v_in.1, ...), custom_call_target="tpu_custom_call" | custom-call | tf_op jit(solution)/shard_map/radial_attention/pallas_call | solution.py:580
  38.0 0.7 %copy.10 = bf16[1,2,64,1280]{3,2,1,0:T(8,128)(2,1)} copy(bf16[1,2,64,1280]{3,2,1,0:T(8,128)(2,1)S(1)} %radial_attention.1) | data formatting | bytes 655360
